TPU v7x, 32 devices: a whole 2x2x4 slice. The times are simulated.
32 devices in a mesh: groups: 2 (over x), ta: 4 (over y, core), xy: 4 (over z).
Axes of the slice: x: 2, y: 2, z: 4, core: 2. Of those that a mesh axis runs over, the one named last changes fastest.
Arguments:
- sources: bfloat16 [8, 4, 4, 8, 96, 256], P('groups', 'ta', 'xy'), parts along dimension 0, may hold values from -24 to 24
- coarse_links: bfloat16 [18, 4, 4, 4, 8, 96, 96], P('groups', None, 'ta', 'xy'), parts along dimension 0, may hold values from -0.119628906 to 0.119628906
Outputs:
- solution: float32 [8, 4, 4, 8, 96, 256], P('groups', 'ta', 'xy'), parts along dimension 0
There are 2 independent parts, one for each index of `groups`. A program takes and returns all parts, laid end to end along the dimension named above; each array names one. Nothing has to cross between parts.
All inputs are finite; a program needn't handle non-finite values.
Results may differ from a plain program's by a relative error of at most 0.0019.
The roundings to bfloat16 on the way count: a program that leaves them out, or rounds other values in their place, can miss the bound.
Values may be sent and summed in bfloat16 or wider, within the bound.
A program may use at most 128 MiB of HBM per device.

v0:
```python
import jax
import jax.numpy as jnp
from jax import lax
from jax.sharding import PartitionSpec as P

ITERS = 2


mass_term = 2.0


def with_halo(cells, sides, width):
    for axis, dim in sides:
        count = lax.axis_size(axis)
        head = lax.slice_in_dim(cells, 0, width, axis=dim)
        tail = lax.slice_in_dim(cells, cells.shape[dim] - width, cells.shape[dim], axis=dim)
        cells = jnp.concatenate(
            [
                lax.ppermute(tail, axis, [(i, (i + 1) % count) for i in range(count)]),
                cells,
                lax.ppermute(head, axis, [((i + 1) % count, i) for i in range(count)]),
            ],
            axis=dim,
        )
    return cells


def link_product(link_field, vector, flipped):
    einsum_form = "abcdio,abcdir->abcdor" if flipped else "abcdoi,abcdir->abcdor"
    return jnp.einsum(einsum_form, link_field, vector, preferred_element_type=jnp.float32)


def widen(vector):
    return with_halo(vector, (("ta", 1), ("xy", 2)), 1)


def apply_forward(rounded, coarse_links):
    padded = widen(rounded)
    neighbours = (
        padded[:, 2:, 1:-1],
        padded[:, :-2, 1:-1],
        padded[:, 1:-1, 2:],
        padded[:, 1:-1, :-2],
        jnp.roll(rounded, -1, 0),
        jnp.roll(rounded, 1, 0),
        jnp.roll(rounded, -1, 3),
        jnp.roll(rounded, 1, 3),
    )
    summed = mass_term * rounded.astype(jnp.float32) + link_product(coarse_links[0], rounded, False)
    for number in range(8):
        summed = summed + link_product(coarse_links[number + 1], neighbours[number], False)
    return summed


def local_adjoint(image_vec, coarse_links):
    summed = mass_term * image_vec.astype(jnp.float32) + link_product(
        coarse_links[0], image_vec, True
    )
    plane_moves = ((4, 1, 0), (5, -1, 0), (6, 1, 3), (7, -1, 3))
    for number, sign_value, axis_number in plane_moves:
        adjoint_term = link_product(coarse_links[number + 1], image_vec, True).astype(jnp.bfloat16)
        summed = summed + jnp.roll(adjoint_term, sign_value, axis_number).astype(jnp.float32)
    return summed


def adjoint_products(image_vec, coarse_links):
    summed = local_adjoint(image_vec, coarse_links)
    adjoint_terms = [
        link_product(coarse_links[number + 1], image_vec, True).astype(jnp.bfloat16)
        for number in range(4)
    ]
    rim_time = jnp.concatenate((adjoint_terms[1], adjoint_terms[0]), axis=1)
    ext_time = with_halo(rim_time, (("ta", 1),), 1)
    rim_space = jnp.concatenate((adjoint_terms[3], adjoint_terms[2]), axis=2)
    ext_space = with_halo(rim_space, (("xy", 2),), 1)
    shifted = (
        jnp.concatenate((ext_time[:, :1], adjoint_terms[0][:, :-1]), axis=1),
        jnp.concatenate((adjoint_terms[1][:, 1:], ext_time[:, -1:]), axis=1),
        jnp.concatenate((ext_space[:, :, :1], adjoint_terms[2][:, :, :-1]), axis=2),
        jnp.concatenate((adjoint_terms[3][:, :, 1:], ext_space[:, :, -1:]), axis=2),
    )
    for moved_term in shifted:
        summed = summed + moved_term.astype(jnp.float32)
    return summed


def gram(left_vec, right_vec):
    left_rows = left_vec.reshape((-1,) + left_vec.shape[-2:])
    right_rows = right_vec.reshape((-1,) + right_vec.shape[-2:])
    return jnp.einsum("sir,sit->rt", left_rows, right_rows, precision=lax.Precision.HIGHEST)


def combine(vector, coefficients):
    return jnp.einsum("abcdir,rt->abcdit", vector, coefficients, precision=lax.Precision.HIGHEST)


def solve_spd(matrix, right_side):
    factor = jnp.linalg.cholesky(matrix)
    return jax.scipy.linalg.cho_solve((factor, True), right_side)


def residual_norms(residual):
    return lax.psum(gram(residual, residual), ("ta", "xy"))


def body(sources, coarse_links):
    residual = sources.astype(jnp.float32)
    solution = jnp.zeros_like(residual)
    search = residual
    energy = residual_norms(residual)
    for iteration in range(ITERS):
        rounded = search.astype(jnp.bfloat16)
        image_vec = apply_forward(rounded, coarse_links).astype(jnp.bfloat16)
        normal_image = adjoint_products(image_vec, coarse_links)
        curvature, cross_term, image_gram = lax.psum(
            (
                gram(search, normal_image),
                gram(residual, normal_image),
                gram(normal_image, normal_image),
            ),
            ("ta", "xy"),
        )
        alpha_step = solve_spd(curvature, energy)
        solution = solution + combine(search, alpha_step)
        if iteration + 1 < ITERS:
            residual = residual - combine(normal_image, alpha_step)
            mixed_term = jnp.dot(cross_term, alpha_step, precision=lax.Precision.HIGHEST)
            quadratic = jnp.dot(
                alpha_step.T,
                jnp.dot(image_gram, alpha_step, precision=lax.Precision.HIGHEST),
                precision=lax.Precision.HIGHEST,
            )
            fresh_energy = energy - mixed_term - mixed_term.T + quadratic
            beta_step = solve_spd(energy, fresh_energy)
            search = residual + combine(search, beta_step)
            energy = fresh_energy
    return solution


def solution(mesh):
    return jax.shard_map(
        body,
        mesh=mesh,
        in_specs=(
            P("groups", "ta", "xy", None, None, None),
            P("groups", None, "ta", "xy", None, None, None),
        ),
        out_specs=P("groups", "ta", "xy", None, None, None),
        check_vma=False,
    )
```

profile of v0, /device:TPU:0, one launch (start us, length us, event | category | flops | bytes accessed | tf_op | source)
XLA Modules:
  0.0 1095.6 jit_solution(8653942792856709858)
XLA Ops:
  9.0 35.1 %collective-permute-done = bf16[4,1,1,8,96,256]{5,4,3,0,2,1:T(8,128)(2,1)S(1)} collective-permute-done((bf16[4,1,1,8,96,256]{5,4,3,0,2,1:T(8,128)(2,1)}, bf16[4,1,1,8,96,256]{5,4,3,0,2,1:T(8,128)(2,1)S(1)}, u32[]{:S(2)}, u32[]{:S(2)}) %collective-permute-start) | collective-permute-done | bytes 1572896 | tf_op jit(solution)/shard_map/ppermute | solution.py:21
  65.1 87.6 %collective-permute-done.2 = bf16[4,3,1,8,96,256]{5,4,3,0,2,1:T(8,128)(2,1)S(1)} collective-permute-done((bf16[4,3,1,8,96,256]{5,4,3,0,2,1:T(8,128)(2,1)S(1)}, bf16[4,3,1,8,96,256]{5,4,3,0,2,1:T(8,128)(2,1)S(1)}, u32[]{:S(2)}, u32[]{:S(2)}) %collective-permute-start.2) | collective-permute-done | bytes 4718624 | tf_op jit(solution)/shard_map/ppermute | solution.py:21
  155.1 98.2 %collective-permute-done.3 = bf16[4,3,1,8,96,256]{5,4,3,0,2,1:T(8,128)(2,1)} collective-permute-done((bf16[4,3,1,8,96,256]{5,4,3,0,2,1:T(8,128)(2,1)S(1)}, bf16[4,3,1,8,96,256]{5,4,3,0,2,1:T(8,128)(2,1)}, u32[]{:S(2)}, u32[]{:S(2)}) %collective-permute-start.3) | collective-permute-done | bytes 4718624 | tf_op jit(solution)/shard_map/ppermute | solution.py:19
  253.2 8.8 fusion.9
  274.3 24.5 %collective-permute-done.4 = bf16[4,1,1,8,96,256]{5,4,3,0,2,1:T(8,128)(2,1)S(1)} collective-permute-done((bf16[4,1,1,8,96,256]{5,4,3,0,2,1:T(8,128)(2,1)S(1)}, bf16[4,1,1,8,96,256]{5,4,3,0,2,1:T(8,128)(2,1)S(1)}, u32[]{:S(2)}, u32[]{:S(2)}) %collective-permute-start.4) | collective-permute-done | bytes 1572896 | tf_op jit(solution)/shard_map/ppermute | solution.py:19
  305.4 33.0 %collective-permute-done.7 = bf16[4,1,1,8,96,256]{5,4,3,0,2,1:T(8,128)(2,1)S(1)} collective-permute-done((bf16[4,1,1,8,96,256]{5,4,3,0,2,1:T(8,128)(2,1)S(1)}, bf16[4,1,1,8,96,256]{5,4,3,0,2,1:T(8,128)(2,1)S(1)}, u32[]{:S(2)}, u32[]{:S(2)}) %collective-permute-start.7) | collective-permute-done | bytes 1572896 | tf_op jit(solution)/shard_map/ppermute | solution.py:21
  344.2 6.4 convolution_bitcast_fusion.3
  350.7 91.8 %all-reduce.7.cloned.1.call-done = (f32[256,256]{0,1:T(8,128)}, f32[256,256]{0,1:T(8,128)}, f32[256,256]{1,0:T(8,128)}) async-done(((f32[256,256]{0,1:T(8,128)}, f32[256,256]{0,1:T(8,128)}, f32[256,256]{1,0:T(8,128)}), (f32[256,256]{0,1:T(8,128)}, f32[256,256]{0,1:T(8,128)}, f32[256,256]{1,0:T(8,128)})) %all-reduce.7.cloned.1.call-update) | async-done | bytes 786448 | tf_op jit(solution)/shard_map/psum | solution.py:103
  444.7 11.7 %cholesky.206 = f32[128,128]{1,0:T(8,128)S(1)} custom-call(f32[128,128]{1,0:T(8,128)S(1)} %cholesky.273), custom_call_target="Cholesky" | custom-call | tf_op jit(solution)/shard_map/jit(cholesky)/cholesky | solution.py:98
  456.5 9.8 custom-call.19
  466.8 11.7 %cholesky.223 = f32[128,128]{1,0:T(8,128)S(1)} custom-call(f32[128,128]{1,0:T(8,128)S(1)} %convolution_subtract_fusion.7), custom_call_target="Cholesky" | custom-call | tf_op jit(solution)/shard_map/jit(cholesky)/cholesky | solution.py:98
  485.6 19.7 %custom-call.20 = f32[2,128,128]{1,2,0:T(8,128)S(1)} custom-call(f32[2,128,128]{2,1,0:T(8,128)S(1)} %get-tuple-element.28), custom_call_target="InvertDiagBlocksLowerTriangular" | custom-call | tf_op jit(solution)/shard_map/jit(_cho_solve)/triangular_solve | solution.py:99
  505.5 11.7 %cholesky.172 = f32[128,128]{1,0:T(8,128)S(1)} custom-call(f32[128,128]{1,0:T(8,128)S(1)} %cholesky.270), custom_call_target="Cholesky" | custom-call | tf_op jit(solution)/shard_map/jit(cholesky)/cholesky | solution.py:98
  517.3 9.8 custom-call.17
  527.6 11.7 %cholesky.189 = f32[128,128]{1,0:T(8,128)S(1)} custom-call(f32[128,128]{1,0:T(8,128)S(1)} %convolution_subtract_fusion.8), custom_call_target="Cholesky" | custom-call | tf_op jit(solution)/shard_map/jit(cholesky)/cholesky | solution.py:98
  545.8 20.1 %custom-call.18 = f32[2,128,128]{1,2,0:T(8,128)S(1)} custom-call(f32[2,128,128]{2,1,0:T(8,128)S(1)} %get-tuple-element.27), custom_call_target="InvertDiagBlocksLowerTriangular" | custom-call | tf_op jit(solution)/shard_map/jit(_cho_solve)/triangular_solve | solution.py:99
  577.7 33.4 %collective-permute-done.8 = bf16[4,1,1,8,96,256]{5,4,3,0,2,1:T(8,128)(2,1)S(1)} collective-permute-done((bf16[4,1,1,8,96,256]{5,4,3,0,2,1:T(8,128)(2,1)S(1)}, bf16[4,1,1,8,96,256]{5,4,3,0,2,1:T(8,128)(2,1)S(1)}, u32[]{:S(2)}, u32[]{:S(2)}) %collective-permute-start.8) | collective-permute-done | bytes 1572896 | tf_op jit(solution)/shard_map/ppermute | solution.py:21
  631.5 86.8 %collective-permute-done.10 = bf16[4,3,1,8,96,256]{5,4,3,0,2,1:T(8,128)(2,1)S(1)} collective-permute-done((bf16[4,3,1,8,96,256]{5,4,3,0,2,1:T(8,128)(2,1)S(1)}, bf16[4,3,1,8,96,256]{5,4,3,0,2,1:T(8,128)(2,1)S(1)}, u32[]{:S(2)}, u32[]{:S(2)}) %collective-permute-start.10) | collective-permute-done | bytes 4718624 | tf_op jit(solution)/shard_map/ppermute | solution.py:21
  720.6 99.8 %collective-permute-done.11 = bf16[4,3,1,8,96,256]{5,4,3,0,2,1:T(8,128)(2,1)} collective-permute-done((bf16[4,3,1,8,96,256]{5,4,3,0,2,1:T(8,128)(2,1)S(1)}, bf16[4,3,1,8,96,256]{5,4,3,0,2,1:T(8,128)(2,1)}, u32[]{:S(2)}, u32[]{:S(2)}) %collective-permute-start.11) | collective-permute-done | bytes 4718624 | tf_op jit(solution)/shard_map/ppermute | solution.py:19
  820.3 9.5 fusion.19
  842.0 29.1 %collective-permute-done.12 = bf16[4,1,1,8,96,256]{5,4,3,0,2,1:T(8,128)(2,1)S(1)} collective-permute-done((bf16[4,1,1,8,96,256]{5,4,3,0,2,1:T(8,128)(2,1)S(1)}, bf16[4,1,1,8,96,256]{5,4,3,0,2,1:T(8,128)(2,1)S(1)}, u32[]{:S(2)}, u32[]{:S(2)}) %collective-permute-start.12) | collective-permute-done | bytes 1572896 | tf_op jit(solution)/shard_map/ppermute | solution.py:19
  871.1 4.6 collective-permute-done.14
  876.9 30.4 %collective-permute-done.15 = bf16[4,1,1,8,96,256]{5,4,3,0,2,1:T(8,128)(2,1)} collective-permute-done((bf16[4,1,1,8,96,256]{5,4,3,0,2,1:T(8,128)(2,1)S(1)}, bf16[4,1,1,8,96,256]{5,4,3,0,2,1:T(8,128)(2,1)}, u32[]{:S(2)}, u32[]{:S(2)}) %collective-permute-start.15) | collective-permute-done | bytes 1572896 | tf_op jit(solution)/shard_map/ppermute | solution.py:21
  907.3 4.7 fusion.18
  912.0 6.0 convolution_bitcast_fusion.2
  921.1 86.1 %all-reduce.5.cloned.1.call-done = f32[256,256]{0,1:T(8,128)} async-done(((f32[256,256]{0,1:T(8,128)}), f32[256,256]{0,1:T(8,128)}) %all-reduce.5.cloned.1.call-update) | async-done | bytes 262160 | tf_op jit(solution)/shard_map/psum | solution.py:115
  1010.8 11.7 %cholesky.240 = f32[128,128]{1,0:T(8,128)S(1)} custom-call(f32[128,128]{1,0:T(8,128)S(1)} %cholesky.276), custom_call_target="Cholesky" | custom-call | tf_op jit(solution)/shard_map/jit(cholesky)/cholesky | solution.py:98
  1023.3 10.0 custom-call.21
  1036.1 11.7 %cholesky.257 = f32[128,128]{1,0:T(8,128)S(1)} custom-call(f32[128,128]{1,0:T(8,128)S(1)} %convolution_subtract_fusion.6), custom_call_target="Cholesky" | custom-call | tf_op jit(solution)/shard_map/jit(cholesky)/cholesky | solution.py:98
  1052.6 5.6 while.8
  1058.8 20.5 %custom-call.22 = f32[2,128,128]{1,2,0:T(8,128)S(1)} custom-call(f32[2,128,128]{2,1,0:T(8,128)} %copy-done.13), custom_call_target="InvertDiagBlocksLowerTriangular" | custom-call | tf_op jit(solution)/shard_map/jit(_cho_solve)/triangular_solve | solution.py:99
  1082.9 5.4 fusion.32
  (217 shorter events, 143.5 us)
Async XLA Ops:
  6.5 436.0 %all-reduce.7.cloned.1.call-start = ((), (), s32[]{:S(2)}) async-start(), calls=%async_computation.1 | async-start | bytes 1572864 | tf_op jit(solution)/shard_map/psum | solution.py:103
  6.5 37.5 %collective-permute-start = (bf16[4,1,1,8,96,256]{5,4,3,0,2,1:T(8,128)(2,1)}, bf16[4,1,1,8,96,256]{5,4,3,0,2,1:T(8,128)(2,1)S(1)}, u32[]{:S(2)}, u32[]{:S(2)}) collective-permute-start(bf16[4,1,1,8,96,256]{5,4,3,0,2,1:T(8,128)(2,1)} %bitcast.587), channel_id=1, source_target_pairs={{4,0},{8,4},{12,8},{0,12},{5,1},{9,5},{13,9},{1,13},{6,2},{10,6},{... | collective-permute-start | bytes 4718600 | tf_op jit(solution)/shard_map/ppermute | solution.py:21
  9.0 36.1 %collective-permute-start.1 = (bf16[4,1,1,8,96,256]{5,4,3,0,2,1:T(8,128)(2,1)}, bf16[4,1,1,8,96,256]{5,4,3,0,2,1:T(8,128)(2,1)S(1)}, u32[]{:S(2)}, u32[]{:S(2)}) collective-permute-start(bf16[4,1,1,8,96,256]{5,4,3,0,2,1:T(8,128)(2,1)} %bitcast.588), channel_id=1, source_target_pairs={{0,4},{4,8},{8,12},{12,0},{1,5},{5,9},{9,13},{13,1},{2,6},{6,10},{... | collective-permute-start | bytes 4718600 | tf_op jit(solution)/shard_map/ppermute | solution.py:19
  46.9 105.9 %collective-permute-start.2 = (bf16[4,3,1,8,96,256]{5,4,3,0,2,1:T(8,128)(2,1)S(1)}, bf16[4,3,1,8,96,256]{5,4,3,0,2,1:T(8,128)(2,1)S(1)}, u32[]{:S(2)}, u32[]{:S(2)}) collective-permute-start(bf16[4,3,1,8,96,256]{5,4,3,0,2,1:T(8,128)(2,1)S(1)} %pad_maximum_fusion), channel_id=1, source_target_pairs={{1,0},{2,1},{3,2},{0,3},{5,4},{6,5},{7,6},{4,7},{9,8},{10,9},{11,1... | collective-permute-start | bytes 14155784 | tf_op jit(solution)/shard_map/ppermute | solution.py:21
  50.6 202.7 %collective-permute-start.3 = (bf16[4,3,1,8,96,256]{5,4,3,0,2,1:T(8,128)(2,1)S(1)}, bf16[4,3,1,8,96,256]{5,4,3,0,2,1:T(8,128)(2,1)}, u32[]{:S(2)}, u32[]{:S(2)}) collective-permute-start(bf16[4,3,1,8,96,256]{5,4,3,0,2,1:T(8,128)(2,1)S(1)} %pad_maximum_fusion), channel_id=1, source_target_pairs={{0,1},{1,2},{2,3},{3,0},{4,5},{5,6},{6,7},{7,4},{8,9},{9,10},{10,1... | collective-permute-start | bytes 14155784 | tf_op jit(solution)/shard_map/ppermute | solution.py:19
  264.5 34.3 %collective-permute-start.4 = (bf16[4,1,1,8,96,256]{5,4,3,0,2,1:T(8,128)(2,1)S(1)}, bf16[4,1,1,8,96,256]{5,4,3,0,2,1:T(8,128)(2,1)S(1)}, u32[]{:S(2)}, u32[]{:S(2)}) collective-permute-start(bf16[4,1,1,8,96,256]{5,4,3,0,2,1:T(8,128)(2,1)S(1)} %fusion.109), channel_id=1, source_target_pairs={{0,4},{4,8},{8,12},{12,0},{1,5},{5,9},{9,13},{13,1},{2,6},{6,10},{... | collective-permute-start | bytes 4718600 | tf_op jit(solution)/shard_map/ppermute | solution.py:19
  264.6 36.4 %collective-permute-start.5 = (bf16[4,1,1,8,96,256]{5,4,3,0,2,1:T(8,128)(2,1)S(1)}, bf16[4,1,1,8,96,256]{5,4,3,0,2,1:T(8,128)(2,1)S(1)}, u32[]{:S(2)}, u32[]{:S(2)}) collective-permute-start(bf16[4,1,1,8,96,256]{5,4,3,0,2,1:T(8,128)(2,1)S(1)} %fusion.112), channel_id=1, source_target_pairs={{4,0},{8,4},{12,8},{0,12},{5,1},{9,5},{13,9},{1,13},{6,2},{10,6},{... | collective-permute-start | bytes 4718600 | tf_op jit(solution)/shard_map/ppermute | solution.py:21
  266.3 39.1 %collective-permute-start.6 = (bf16[4,1,1,8,96,256]{5,4,3,0,2,1:T(8,128)(2,1)S(1)}, bf16[4,1,1,8,96,256]{5,4,3,0,2,1:T(8,128)(2,1)S(1)}, u32[]{:S(2)}, u32[]{:S(2)}) collective-permute-start(bf16[4,1,1,8,96,256]{5,4,3,0,2,1:T(8,128)(2,1)S(1)} %fusion.115), channel_id=1, source_target_pairs={{0,1},{1,2},{2,3},{3,0},{4,5},{5,6},{6,7},{7,4},{8,9},{9,10},{10,1... | collective-permute-start | bytes 4718600 | tf_op jit(solution)/shard_map/ppermute | solution.py:19
  267.9 70.5 %collective-permute-start.7 = (bf16[4,1,1,8,96,256]{5,4,3,0,2,1:T(8,128)(2,1)S(1)}, bf16[4,1,1,8,96,256]{5,4,3,0,2,1:T(8,128)(2,1)S(1)}, u32[]{:S(2)}, u32[]{:S(2)}) collective-permute-start(bf16[4,1,1,8,96,256]{5,4,3,0,2,1:T(8,128)(2,1)S(1)} %fusion.118), channel_id=1, source_target_pairs={{1,0},{2,1},{3,2},{0,3},{5,4},{6,5},{7,6},{4,7},{9,8},{10,9},{11,1... | collective-permute-start | bytes 4718600 | tf_op jit(solution)/shard_map/ppermute | solution.py:21
  273.9 64.5 %slice-start.8 = ((bf16[4,1,1,8,96,256]{5,4,3,0,2,1:T(8,128)(2,1)}), bf16[4,1,1,7,96,256]{5,4,3,0,2,1:T(8,128)(2,1)S(1)}, s32[]{:S(2)}) async-start(bf16[4,1,1,8,96,256]{5,4,3,0,2,1:T(8,128)(2,1)} %copy-done.7), calls=%async_computation.10 | async-start | bytes 2752512 | tf_op jit(solution)/shard_map/jit(_roll_static)/slice | solution.py:62
  273.9 64.5 %slice-start.9 = ((bf16[4,1,1,8,96,256]{5,4,3,0,2,1:T(8,128)(2,1)}), bf16[4,1,1,1,96,256]{5,4,3,0,2,1:T(8,128)(2,1)S(1)}, s32[]{:S(2)}) async-start(bf16[4,1,1,8,96,256]{5,4,3,0,2,1:T(8,128)(2,1)} %copy-done.7), calls=%async_computation.11 | async-start | bytes 393216 | tf_op jit(solution)/shard_map/jit(_roll_static)/slice | solution.py:62
  273.9 64.5 %slice-start.10 = ((bf16[4,1,1,8,96,256]{5,4,3,0,2,1:T(8,128)(2,1)}), bf16[4,1,1,7,96,256]{5,4,3,0,2,1:T(8,128)(2,1)S(1)}, s32[]{:S(2)}) async-start(bf16[4,1,1,8,96,256]{5,4,3,0,2,1:T(8,128)(2,1)} %copy-done.8), calls=%async_computation.12 | async-start | bytes 2752512 | tf_op jit(solution)/shard_map/jit(_roll_static)/slice | solution.py:62
  273.9 64.5 %slice-start.11 = ((bf16[4,1,1,8,96,256]{5,4,3,0,2,1:T(8,128)(2,1)}), bf16[4,1,1,1,96,256]{5,4,3,0,2,1:T(8,128)(2,1)S(1)}, s32[]{:S(2)}) async-start(bf16[4,1,1,8,96,256]{5,4,3,0,2,1:T(8,128)(2,1)} %copy-done.8), calls=%async_computation.13 | async-start | bytes 393216 | tf_op jit(solution)/shard_map/jit(_roll_static)/slice | solution.py:62
  350.7 656.6 %all-reduce.5.cloned.1.call-start = ((), (), s32[]{:S(2)}) async-start(), calls=%async_computation | async-start | bytes 524288 | tf_op jit(solution)/shard_map/psum | solution.py:115
  442.6 62.7 %copy-start.10 = (f32[256,256]{0,1:T(8,128)S(1)}, f32[256,256]{0,1:T(8,128)}, u32[]{:S(2)}) copy-start(f32[256,256]{0,1:T(8,128)} %get-tuple-element.55) | copy-start | bytes 786436
  456.5 109.5 %copy-start.9 = (f32[256,256]{0,1:T(8,128)S(1)}, f32[256,256]{0,1:T(8,128)}, u32[]{:S(2)}) copy-start(f32[256,256]{0,1:T(8,128)} %get-tuple-element.54) | copy-start | bytes 786436
  505.5 63.1 %copy-start.12 = (f32[256,256]{1,0:T(8,128)S(1)}, f32[256,256]{1,0:T(8,128)}, u32[]{:S(2)}) copy-start(f32[256,256]{1,0:T(8,128)} %get-tuple-element.56) | copy-start | bytes 786436
  572.9 44.1 %slice-start.2 = ((s8[7077888]{0:T(1024)(128)(4,1)}), s8[4194304]{0:T(1024)(128)(4,1)S(1)}, s32[]{:S(2)}) async-start(s8[7077888]{0:T(1024)(128)(4,1)} %bitcast.616), calls=%async_computation.4 | async-start | bytes 8388608
  577.2 33.9 %collective-permute-start.8 = (bf16[4,1,1,8,96,256]{5,4,3,0,2,1:T(8,128)(2,1)S(1)}, bf16[4,1,1,8,96,256]{5,4,3,0,2,1:T(8,128)(2,1)S(1)}, u32[]{:S(2)}, u32[]{:S(2)}) collective-permute-start(bf16[4,1,1,8,96,256]{5,4,3,0,2,1:T(8,128)(2,1)S(1)} %get-tuple-element.95), channel_id=1, source_target_pairs={{4,0},{8,4},{12,8},{0,12},{5,1},{9,5},{13,9},{1,13},{6,2},{10,6},{... | collective-permute-start | bytes 4718600 | tf_op jit(solution)/shard_map/ppermute | solution.py:21
  577.2 36.7 %collective-permute-start.9 = (bf16[4,1,1,8,96,256]{5,4,3,0,2,1:T(8,128)(2,1)S(1)}, bf16[4,1,1,8,96,256]{5,4,3,0,2,1:T(8,128)(2,1)S(1)}, u32[]{:S(2)}, u32[]{:S(2)}) collective-permute-start(bf16[4,1,1,8,96,256]{5,4,3,0,2,1:T(8,128)(2,1)S(1)} %get-tuple-element.95), channel_id=1, source_target_pairs={{0,4},{4,8},{8,12},{12,0},{1,5},{5,9},{9,13},{13,1},{2,6},{6,10},{... | collective-permute-start | bytes 4718600 | tf_op jit(solution)/shard_map/ppermute | solution.py:19
  614.4 103.9 %collective-permute-start.10 = (bf16[4,3,1,8,96,256]{5,4,3,0,2,1:T(8,128)(2,1)S(1)}, bf16[4,3,1,8,96,256]{5,4,3,0,2,1:T(8,128)(2,1)S(1)}, u32[]{:S(2)}, u32[]{:S(2)}) collective-permute-start(bf16[4,3,1,8,96,256]{5,4,3,0,2,1:T(8,128)(2,1)S(1)} %pad_maximum_fusion.1), channel_id=1, source_target_pairs={{1,0},{2,1},{3,2},{0,3},{5,4},{6,5},{7,6},{4,7},{9,8},{10,9},{11,1... | collective-permute-start | bytes 14155784 | tf_op jit(solution)/shard_map/ppermute | solution.py:21
  615.8 204.5 %collective-permute-start.11 = (bf16[4,3,1,8,96,256]{5,4,3,0,2,1:T(8,128)(2,1)S(1)}, bf16[4,3,1,8,96,256]{5,4,3,0,2,1:T(8,128)(2,1)}, u32[]{:S(2)}, u32[]{:S(2)}) collective-permute-start(bf16[4,3,1,8,96,256]{5,4,3,0,2,1:T(8,128)(2,1)S(1)} %pad_maximum_fusion.1), channel_id=1, source_target_pairs={{0,1},{1,2},{2,3},{3,0},{4,5},{5,6},{6,7},{7,4},{8,9},{9,10},{10,1... | collective-permute-start | bytes 14155784 | tf_op jit(solution)/shard_map/ppermute | solution.py:19
  834.9 36.2 %collective-permute-start.12 = (bf16[4,1,1,8,96,256]{5,4,3,0,2,1:T(8,128)(2,1)S(1)}, bf16[4,1,1,8,96,256]{5,4,3,0,2,1:T(8,128)(2,1)S(1)}, u32[]{:S(2)}, u32[]{:S(2)}) collective-permute-start(bf16[4,1,1,8,96,256]{5,4,3,0,2,1:T(8,128)(2,1)S(1)} %fusion.133), channel_id=1, source_target_pairs={{0,4},{4,8},{8,12},{12,0},{1,5},{5,9},{9,13},{13,1},{2,6},{6,10},{... | collective-permute-start | bytes 4718600 | tf_op jit(solution)/shard_map/ppermute | solution.py:19
  834.9 36.2 %collective-permute-start.13 = (bf16[4,1,1,8,96,256]{5,4,3,0,2,1:T(8,128)(2,1)S(1)}, bf16[4,1,1,8,96,256]{5,4,3,0,2,1:T(8,128)(2,1)S(1)}, u32[]{:S(2)}, u32[]{:S(2)}) collective-permute-start(bf16[4,1,1,8,96,256]{5,4,3,0,2,1:T(8,128)(2,1)S(1)} %fusion.136), channel_id=1, source_target_pairs={{4,0},{8,4},{12,8},{0,12},{5,1},{9,5},{13,9},{1,13},{6,2},{10,6},{... | collective-permute-start | bytes 4718600 | tf_op jit(solution)/shard_map/ppermute | solution.py:21
  836.6 39.1 %collective-permute-start.14 = (bf16[4,1,1,8,96,256]{5,4,3,0,2,1:T(8,128)(2,1)S(1)}, bf16[4,1,1,8,96,256]{5,4,3,0,2,1:T(8,128)(2,1)S(1)}, u32[]{:S(2)}, u32[]{:S(2)}) collective-permute-start(bf16[4,1,1,8,96,256]{5,4,3,0,2,1:T(8,128)(2,1)S(1)} %fusion.139), channel_id=1, source_target_pairs={{0,1},{1,2},{2,3},{3,0},{4,5},{5,6},{6,7},{7,4},{8,9},{9,10},{10,1... | collective-permute-start | bytes 4718600 | tf_op jit(solution)/shard_map/ppermute | solution.py:19
  836.6 70.6 %collective-permute-start.15 = (bf16[4,1,1,8,96,256]{5,4,3,0,2,1:T(8,128)(2,1)S(1)}, bf16[4,1,1,8,96,256]{5,4,3,0,2,1:T(8,128)(2,1)}, u32[]{:S(2)}, u32[]{:S(2)}) collective-permute-start(bf16[4,1,1,8,96,256]{5,4,3,0,2,1:T(8,128)(2,1)S(1)} %fusion.142), channel_id=1, source_target_pairs={{1,0},{2,1},{3,2},{0,3},{5,4},{6,5},{7,6},{4,7},{9,8},{10,9},{11,1... | collective-permute-start | bytes 4718600 | tf_op jit(solution)/shard_map/ppermute | solution.py:21
  841.7 65.5 %slice-start.4 = ((bf16[4,1,1,8,96,256]{5,4,3,0,2,1:T(8,128)(2,1)}), bf16[4,1,1,7,96,256]{5,4,3,0,2,1:T(8,128)(2,1)S(1)}, s32[]{:S(2)}) async-start(bf16[4,1,1,8,96,256]{5,4,3,0,2,1:T(8,128)(2,1)} %copy-done.5), calls=%async_computation.6 | async-start | bytes 2752512 | tf_op jit(solution)/shard_map/jit(_roll_static)/slice | solution.py:62
  841.7 65.5 %slice-start.5 = ((bf16[4,1,1,8,96,256]{5,4,3,0,2,1:T(8,128)(2,1)}), bf16[4,1,1,1,96,256]{5,4,3,0,2,1:T(8,128)(2,1)S(1)}, s32[]{:S(2)}) async-start(bf16[4,1,1,8,96,256]{5,4,3,0,2,1:T(8,128)(2,1)} %copy-done.5), calls=%async_computation.7 | async-start | bytes 393216 | tf_op jit(solution)/shard_map/jit(_roll_static)/slice | solution.py:62
  841.8 65.5 %slice-start.6 = ((bf16[4,1,1,8,96,256]{5,4,3,0,2,1:T(8,128)(2,1)}), bf16[4,1,1,7,96,256]{5,4,3,0,2,1:T(8,128)(2,1)S(1)}, s32[]{:S(2)}) async-start(bf16[4,1,1,8,96,256]{5,4,3,0,2,1:T(8,128)(2,1)} %copy-done.6), calls=%async_computation.8 | async-start | bytes 2752512 | tf_op jit(solution)/shard_map/jit(_roll_static)/slice | solution.py:62
  841.8 65.5 %slice-start.7 = ((bf16[4,1,1,8,96,256]{5,4,3,0,2,1:T(8,128)(2,1)}), bf16[4,1,1,1,96,256]{5,4,3,0,2,1:T(8,128)(2,1)S(1)}, s32[]{:S(2)}) async-start(bf16[4,1,1,8,96,256]{5,4,3,0,2,1:T(8,128)(2,1)} %copy-done.6), calls=%async_computation.9 | async-start | bytes 393216 | tf_op jit(solution)/shard_map/jit(_roll_static)/slice | solution.py:62
  842.0 70.0 %copy-start.3 = (f32[4,1,1,8,96,256]{5,4,3,0,2,1:T(8,128)S(1)}, f32[4,1,1,8,96,256]{5,4,3,0,2,1:T(8,128)}, u32[]{:S(2)}) copy-start(f32[4,1,1,8,96,256]{5,4,3,0,2,1:T(8,128)} %get-tuple-element.96) | copy-start | bytes 9437188
  921.1 161.8 %copy-start.4 = (f32[4,1,1,8,96,256]{5,4,3,0,2,1:T(8,128)S(1)}, f32[4,1,1,8,96,256]{5,4,3,0,2,1:T(8,128)}, u32[]{:S(2)}) copy-start(f32[4,1,1,8,96,256]{5,4,3,0,2,1:T(8,128)} %get-tuple-element.96) | copy-start | bytes 9437188
  (14 other events, 114.5 us)
Sparse Core Ops, SparseCore 0:
  350.8 91.7 all-reduce.6
  918.1 89.0 all-reduce.4
where the time goes:
time: 1100 us
  waiting for transfers between devices  751 us (68%)
  other arithmetic  171 us (16%)
  matrix products  110 us (10%)
  local copies, waits for them, and re-layouts  24.2 us (2%)
  starting transfers between devices  20.3 us (2%)
  between operations  18.5 us (2%)
    ppermute x8, waiting for transfers between devices, with_halo(): lax.ppermute(head, axis, [((i + 1) % count, i) for i in range(count)])  308 us
    ppermute x8, waiting for transfers between devices, with_halo(): lax.ppermute(tail, axis, [(i, (i + 1) % count) for i in range(count)])  264 us
    another operation x21, other arithmetic, solve_spd(): factor = jnp.linalg.cholesky(matrix)  105 us
    psum x1, waiting for transfers between devices, residual_norms(): return lax.psum(gram(residual, residual), ('ta', 'xy'))  91.8 us
    psum x1, waiting for transfers between devices, body(): lax.psum((gram(search, normal_image), gram(residual, normal_image), gram(...  86.1 us
    dot_general x36, matrix products, link_product(): jnp.einsum(einsum_form, link_field, vector, preferred_element_type=jnp.fl...  66.3 us
    another operation x7, other arithmetic, solve_spd(): return jax.scipy.linalg.cho_solve((factor, True), right_side)  62 us
  transfers between devices with their start and end apart: 18, of which 17 were waited for; matrix products, arithmetic and copies ran while one was open for 4% of the time, Pallas kernels for 0%

commit v1 on v0

v1 whole, which is shorter than its diff:
```python
import functools

import jax
import jax.numpy as jnp
from jax import lax
from jax.experimental import pallas as pl
from jax.experimental.pallas import tpu as pltpu
from jax.sharding import PartitionSpec as P

ITERS = 2
mass_term = 2.0
MESH = pl.DeviceIdType.MESH
HI = lax.Precision.HIGHEST
f32 = jnp.float32
bf16 = jnp.bfloat16


def sum_kernel(n_ta, n_xy, x_ref, o_ref, parts, whole, send1, recv1, send2, recv2):
    n = n_ta * n_xy
    me = lax.axis_index("ta") * n_xy + lax.axis_index("xy")

    def device(off):
        peer = lax.rem(me + off, n)
        return peer, {"ta": peer // n_xy, "xy": lax.rem(peer, n_xy)}

    def first(off):
        peer, where = device(off)
        return pltpu.make_async_remote_copy(
            src_ref=x_ref.at[peer], dst_ref=parts.at[off], send_sem=send1.at[off],
            recv_sem=recv1.at[off], device_id=where, device_id_type=MESH)

    def second(off):
        _, where = device(off)
        return pltpu.make_async_remote_copy(
            src_ref=whole.at[me], dst_ref=whole.at[me], send_sem=send2.at[off],
            recv_sem=recv2.at[off], device_id=where, device_id_type=MESH)

    def arrived(off):
        peer = lax.rem(me + n - off, n)
        return pltpu.make_async_remote_copy(
            src_ref=whole.at[peer], dst_ref=whole.at[peer], send_sem=send2.at[off],
            recv_sem=recv2.at[off], device_id=device(off)[1], device_id_type=MESH)

    barrier = pltpu.get_barrier_semaphore()

    @pl.loop(1, n)
    def _(off):
        pl.semaphore_signal(barrier, inc=1, device_id=device(off)[1], device_id_type=MESH)

    pl.semaphore_wait(barrier, n - 1)

    @pl.loop(1, n)
    def _(off):
        first(off).start()

    @pl.loop(1, n)
    def _(off):
        first(off).wait_recv()

    acc = x_ref[me]
    for off in range(1, n):
        acc = acc + parts[off]
    whole[me] = acc

    @pl.loop(1, n)
    def _(off):
        second(off).start()

    @pl.loop(1, n)
    def _(off):
        arrived(off).wait_recv()

    o_ref[...] = whole[...]

    @pl.loop(1, n)
    def _(off):
        first(off).wait_send()
        second(off).wait_send()


def all_sum(matrix):
    n_ta, n_xy = lax.axis_size("ta"), lax.axis_size("xy")
    n = n_ta * n_xy
    rows, cols = matrix.shape
    per = -(-rows // n)
    padded = jnp.pad(matrix, ((0, per * n - rows), (0, 0))) if per * n != rows else matrix
    shape = (n, per, cols)
    out = pl.pallas_call(
        functools.partial(sum_kernel, n_ta, n_xy),
        out_shape=jax.ShapeDtypeStruct(shape, f32),
        in_specs=[pl.BlockSpec(memory_space=pltpu.VMEM)],
        out_specs=pl.BlockSpec(memory_space=pltpu.VMEM),
        scratch_shapes=[pltpu.VMEM(shape, f32), pltpu.VMEM(shape, f32)]
        + [pltpu.SemaphoreType.DMA((n,))] * 4,
        compiler_params=pltpu.CompilerParams(collective_id=0, has_side_effects=True),
    )(padded.reshape(shape))
    return out.reshape(n * per, cols)[:rows]


def inverse_kernel(a_ref, x_ref, s_ref):
    n = a_ref.shape[0]
    dot = functools.partial(jnp.dot, precision=HI, preferred_element_type=f32)
    row = lax.broadcasted_iota(jnp.int32, (n, n), 0)
    col = lax.broadcasted_iota(jnp.int32, (n, n), 1)
    eye = jnp.where(row == col, 1.0, 0.0).astype(f32)
    a = a_ref[...]
    a = 0.5 * (a + a.T)
    diag = a * eye
    down = lax.rsqrt(jnp.sum(diag, axis=1, keepdims=True))
    across = lax.rsqrt(jnp.sum(diag, axis=0, keepdims=True))
    a = a * down * across
    s_ref[...] = a
    power = eye - a
    x = eye + power
    for _ in range(3):
        power = dot(power, power)
        x = x + dot(x, power)
    x_ref[...] = x
    left = eye - dot(a, x)
    worst = jnp.max(jnp.abs(left))

    @pl.when(jnp.logical_not(worst < 1e-3))
    def _():
        x_ref[...] = s_ref[...]

        def eliminate(k, carry):
            m = x_ref[...]
            pivot_row = x_ref[pl.ds(k, 1), :]
            here = col == k
            pivot_col = jnp.sum(jnp.where(here, m, 0.0), axis=1, keepdims=True)
            hit = here[:1]
            inv = 1.0 / jnp.sum(jnp.where(hit, pivot_row, 0.0), axis=1, keepdims=True)
            scaled = jnp.where(hit, inv, pivot_row * inv)
            m = jnp.where(here, 0.0, m) - pivot_col * scaled
            x_ref[...] = jnp.where(row == k, scaled, m)
            return carry

        lax.fori_loop(0, n, eliminate, 0)

    x = x_ref[...]
    x = x + dot(x, eye - dot(s_ref[...], x))
    x_ref[...] = x * down * across


def spd_inverse(matrix):
    spec = pl.BlockSpec(memory_space=pltpu.VMEM)
    return pl.pallas_call(
        inverse_kernel,
        out_shape=jax.ShapeDtypeStruct(matrix.shape, f32),
        in_specs=[spec],
        out_specs=spec,
        scratch_shapes=[pltpu.VMEM(matrix.shape, f32)],
        cost_estimate=pl.CostEstimate(flops=int(1.5e9), bytes_accessed=1 << 20, transcendentals=0),
    )(matrix)


def mm(a, b):
    return jnp.dot(a, b, precision=HI)


def solve(matrix, inverse, right):
    out = mm(inverse, right)
    sym = 0.5 * (matrix + matrix.T)
    return out + mm(inverse, right - mm(sym, out))


def link_product(link_field, vector, flipped):
    einsum_form = "abcdio,abcdir->abcdor" if flipped else "abcdoi,abcdir->abcdor"
    return jnp.einsum(einsum_form, link_field, vector, preferred_element_type=f32)


def shifted(vector, axis, dim, step):
    count, size = lax.axis_size(axis), vector.shape[dim]
    if step > 0:
        edge = lax.slice_in_dim(vector, 0, 1, axis=dim)
        came = lax.ppermute(edge, axis, [((i + 1) % count, i) for i in range(count)])
        rest = [lax.slice_in_dim(vector, 1, size, axis=dim)] if size > 1 else []
        pieces = rest + [came]
    else:
        edge = lax.slice_in_dim(vector, size - 1, size, axis=dim)
        came = lax.ppermute(edge, axis, [(i, (i + 1) % count) for i in range(count)])
        rest = [lax.slice_in_dim(vector, 0, size - 1, axis=dim)] if size > 1 else []
        pieces = [came] + rest
    return jnp.concatenate(pieces, axis=dim) if len(pieces) > 1 else pieces[0]


HOPS = (("ta", 1, 1), ("ta", 1, -1), ("xy", 2, 1), ("xy", 2, -1))
LOCAL = ((0, 1), (0, -1), (3, 1), (3, -1))


def apply_forward(rounded, links):
    far = [shifted(rounded, *hop) for hop in HOPS]
    total = mass_term * rounded.astype(f32) + link_product(links[0], rounded, False)
    for number, (dim, step) in enumerate(LOCAL):
        total = total + link_product(links[number + 5], jnp.roll(rounded, -step, dim), False)
    for number in range(4):
        total = total + link_product(links[number + 1], far[number], False)
    return total


def apply_adjoint(image, links):
    sent = [link_product(links[number + 1], image, True).astype(bf16) for number in range(4)]
    far = [shifted(sent[number], axis, dim, -step) for number, (axis, dim, step) in enumerate(HOPS)]
    total = mass_term * image.astype(f32) + link_product(links[0], image, True)
    for number, (dim, step) in enumerate(LOCAL):
        term = link_product(links[number + 5], image, True).astype(bf16)
        total = total + jnp.roll(term, step, dim).astype(f32)
    return total, far


def rows_of(vector):
    return vector.reshape((-1,) + vector.shape[-2:])


def gram(left, right, precision=None):
    return jnp.einsum("sir,sit->rt", rows_of(left), rows_of(right), precision=precision,
                      preferred_element_type=f32)


def image_gram(full, image):
    low = (full - image.astype(f32)).astype(bf16)
    return gram(image, image) + gram(low, image)


def combine(vector, coefficients):
    return jnp.einsum("abcdir,rt->abcdit", vector, coefficients, precision=HI,
                      preferred_element_type=f32)


def body(sources, links):
    residual = sources.astype(f32)
    energy = all_sum(gram(sources, sources))
    energy_inv = spd_inverse(energy)
    search = residual
    solution = None
    for iteration in range(ITERS):
        rounded = search.astype(bf16)
        full = apply_forward(rounded, links)
        image = full.astype(bf16)
        last = iteration + 1 == ITERS
        if not last:
            partial, far = apply_adjoint(image, links)
        curvature = all_sum(image_gram(full, image))
        alpha = solve(curvature, spd_inverse(curvature), energy)
        step = combine(search, alpha)
        solution = step if solution is None else solution + step
        if not last:
            for term in far:
                partial = partial + term.astype(f32)
            residual = residual - combine(partial, alpha)
            fresh = all_sum(gram(residual, residual, HI))
            beta = solve(energy, energy_inv, fresh)
            search = residual + combine(search, beta)
            energy = fresh
    return solution


def solution(mesh):
    return jax.shard_map(
        body,
        mesh=mesh,
        in_specs=(
            P("groups", "ta", "xy", None, None, None),
            P("groups", None, "ta", "xy", None, None, None),
        ),
        out_specs=P("groups", "ta", "xy", None, None, None),
        check_vma=False,
    )
```

time: 1100 us -> 518 us (0.47)
  waiting for transfers between devices: 751 us -> 111 us
  Pallas kernels: 0 us -> 239 us
  other arithmetic: 171 us -> 0.01 us
  between operations: 18.5 us -> 1.03 us
  matrix products: 110 us -> 121 us
    ppermute x16 -> x12, waiting for transfers between devices: 573 us -> 111 us  [the longest x6 55.5 us: shifted(): lax.ppermute(edge, axis, [((i + 1) % count, i) for i in range(count)])]
    pallas_call x0 -> x7, Pallas kernels: none -> 239 us  [the longest x3 123 us: spd_inverse(): pl.pallas_call(inverse_kernel, out_shape=jax.ShapeDtypeStruct(matrix.shap...]
    psum x2 -> x0, waiting for transfers between devices: 178 us -> none  [the longest x1 91.8 us: residual_norms(): return lax.psum(gram(residual, residual), ('ta', 'xy'))]
    another operation x28 -> x0, other arithmetic: 167 us -> none  [the longest x21 105 us: solve_spd(): factor = jnp.linalg.cholesky(matrix)]
    dot_general x47 -> x46, matrix products: 99.3 us -> 121 us  [the longest x27 76.6 us: link_product(): jnp.einsum(einsum_form, link_field, vector, preferred_element_type=f32)]
    another operation x28 -> x0, local copies, waits for them, and re-layouts: 14.3 us -> none  [the longest x22 13.5 us: solve_spd(): return jax.scipy.linalg.cho_solve((factor, True), right_side)]
    reshape x0 -> x5, local copies, waits for them, and re-layouts: none -> 12.1 us  [the longest x2 9.4 us: rows_of(): return vector.reshape((-1,) + vector.shape[-2:])]
  transfers between devices with their start and end apart: 18 -> 12, of which waited for: 17 -> 5; matrix products, arithmetic and copies ran while one was open for 4% -> 13% of each run, Pallas kernels for 0% -> 19%
where the time goes in v1:
time: 518 us; the launch traced here: 512 us
  Pallas kernels  239 us (46%)
  matrix products  121 us (23%)
  waiting for transfers between devices  111 us (21%)
  local copies, waits for them, and re-layouts  23.1 us (4%)
  starting transfers between devices  16.5 us (3%)
    pallas_call x3, Pallas kernels, spd_inverse(): pl.pallas_call(inverse_kernel, out_shape=jax.ShapeDtypeStruct(matrix.shap...  123 us
    pallas_call x4, Pallas kernels, all_sum(): pl.pallas_call(functools.partial(sum_kernel, n_ta, n_xy), out_shape=jax.S...  116 us
    dot_general x27, matrix products, link_product(): jnp.einsum(einsum_form, link_field, vector, preferred_element_type=f32)  76.6 us
    ppermute x6, waiting for transfers between devices, shifted(): lax.ppermute(edge, axis, [((i + 1) % count, i) for i in range(count)])  55.5 us
    ppermute x6, waiting for transfers between devices, shifted(): lax.ppermute(edge, axis, [(i, (i + 1) % count) for i in range(count)])  55.1 us
    dot_general x6, matrix products, gram(): jnp.einsum('sir,sit->rt', rows_of(left), rows_of(right), precision=precis...  19.3 us
    dot_general x4, matrix products, combine(): jnp.einsum('abcdir,rt->abcdit', vector, coefficients, precision=HI, prefe...  18.4 us
    ppermute x6, starting transfers between devices, shifted(): lax.ppermute(edge, axis, [((i + 1) % count, i) for i in range(count)])  14.9 us
  transfers between devices with their start and end apart: 12, of which 5 were waited for; matrix products, arithmetic and copies ran while one was open for 13% of the time, Pallas kernels for 19%

profile of v1, /device:TPU:0, one launch (start us, length us, event | category | flops | bytes accessed | tf_op | source)
XLA Modules:
  0.0 511.7 jit_solution(1380136558767739205)
XLA Ops:
  2.5 4.3 collective-permute-start.2
  6.8 3.4 fusion.174
  15.5 4.2 copy.67
  19.7 4.3 fusion.138.x_ref
  24.0 3.4 fusion.42
  27.4 3.5 fusion.45
  30.9 3.4 fusion.48
  34.4 55.1 %shard_map.30 = f32[16,16,256]{2,1,0:T(8,128)} custom-call(f32[16,16,256]{2,1,0:T(8,128)} %fusion.138.x_ref), custom_call_target="tpu_custom_call" | custom-call | tf_op jit(solution)/shard_map/pallas_call | solution.py:88
  91.2 3.4 fusion.51
  94.6 41.3 %shard_map.31 = f32[256,256]{1,0:T(8,128)} custom-call(f32[256,256]{1,0:T(8,128)} %bitcast.469), custom_call_target="tpu_custom_call" | custom-call | flops 1500000000 | bytes 1048576 | tf_op jit(solution)/shard_map/pallas_call | solution.py:147
  137.6 4.1 fusion.101
  141.8 4.0 fusion.103
  145.8 4.0 fusion.99
  149.8 8.0 %fusion.11 = (bf16[4,1,1,8,96,256]{5,4,3,0,2,1:T(8,128)(2,1)}, bf16[4,1,1,8,96,256]{5,4,3,0,2,1:T(8,128)(2,1)S(1)}) fusion(bf16[4,1,1,8,96,256]{5,4,3,0,2,1:T(8,128)(2,1)} %collective-permute-done.3, bf16[9,4,1,1,8,96,96]{6,5,4,1,3,2,0:T(8,128)(2,1)} %bitcast.438, f32[4,8,96,256]{3,2,1,0:T(8,128)} %fusion.99, f32[4,8,96,256]{3,2,1,0:T(8,128)} %fusion.101, ...), kind=kOutput, calls=%fused_computation.15 | convolution fusion | flops 162791424 | bytes 32243712 | tf_op jit(solution)/shard_map/abcdoi,abcdir->abcdor/dot_general | solution.py:169
  162.8 19.9 %shard_map.28 = f32[16,16,256]{2,1,0:T(8,128)} custom-call(f32[16,16,256]{2,1,0:T(8,128)} %bitcast.484), custom_call_target="tpu_custom_call" | custom-call | tf_op jit(solution)/shard_map/pallas_call | solution.py:88
  182.7 41.0 %shard_map.29 = f32[256,256]{1,0:T(8,128)} custom-call(f32[256,256]{1,0:T(8,128)} %bitcast.473), custom_call_target="tpu_custom_call" | custom-call | flops 1500000000 | bytes 1048576 | tf_op jit(solution)/shard_map/pallas_call | solution.py:147
  240.9 3.1 collective-permute-start.7
  246.0 3.1 fusion.106
  251.0 22.9 %collective-permute-done.4 = bf16[4,1,1,8,96,256]{5,4,3,0,2,1:T(8,128)(2,1)S(1)} collective-permute-done((bf16[4,1,1,8,96,256]{5,4,3,0,2,1:T(8,128)(2,1)S(1)}, bf16[4,1,1,8,96,256]{5,4,3,0,2,1:T(8,128)(2,1)S(1)}, u32[]{:S(2)}, u32[]{:S(2)}) %collective-permute-start.4) | collective-permute-done | bytes 1572896 | tf_op jit(solution)/shard_map/ppermute | solution.py:181
  273.9 5.3 %collective-permute-done.6 = bf16[4,1,1,8,96,256]{5,4,3,0,2,1:T(8,128)(2,1)S(1)} collective-permute-done((bf16[4,1,1,8,96,256]{5,4,3,0,2,1:T(8,128)(2,1)S(1)}, bf16[4,1,1,8,96,256]{5,4,3,0,2,1:T(8,128)(2,1)S(1)}, u32[]{:S(2)}, u32[]{:S(2)}) %collective-permute-start.6) | collective-permute-done | bytes 1572896 | tf_op jit(solution)/shard_map/ppermute | solution.py:181
  279.2 30.7 %collective-permute-done.7 = bf16[4,1,1,8,96,256]{5,4,3,0,2,1:T(8,128)(2,1)S(1)} collective-permute-done((bf16[4,1,1,8,96,256]{5,4,3,0,2,1:T(8,128)(2,1)S(1)}, bf16[4,1,1,8,96,256]{5,4,3,0,2,1:T(8,128)(2,1)S(1)}, u32[]{:S(2)}, u32[]{:S(2)}) %collective-permute-start.7) | collective-permute-done | bytes 1572896 | tf_op jit(solution)/shard_map/ppermute | solution.py:176
  309.9 5.9 %convert_subtract_fusion.1 = f32[4,1,1,8,96,256]{5,4,3,0,2,1:T(8,128)} fusion(f32[256,256,1,1]{1,0,3,2:T(8,128)S(1)} %fusion.137, bf16[4,1,1,8,96,256]{5,4,3,0,2,1:T(8,128)(2,1)S(1)} %get-tuple-element.8, f32[4,8,256,96]{2,3,1,0:T(8,128)S(1)} %fusion.95, bf16[4,1,1,8,96,256]{5,4,3,0,2,1:T(8,128)(2,1)S(1)} %collective-permute-done.7, ...), kind=kOutput, calls=%fused_computation.4 | convolution fusion | flops 2435579904 | bytes 22282240 | tf_op jit(solution)/shard_map/abcdir,rt->abcdit/dot_general | solution.py:226
  315.9 5.2 %copy.79 = f32[32,96,256]{1,0,2:T(8,128)} copy(f32[32,96,256]{2,1,0:T(8,128)} %bitcast.459) | data formatting | bytes 6291456 | tf_op jit(solution)/shard_map/reshape | solution.py:212
  321.0 9.8 %fusion.143.x_ref = f32[16,16,256]{2,1,0:T(8,128)} fusion(f32[32,96,256,1]{2,1,0,3:T(8,128)} %bitcast.460, f32[16,16,96,32]{2,3,1,0:T(8,128)} %bitcast.461), kind=kOutput, calls=%fused_computation.162 | convolution fusion | flops 2415919104 | bytes 6553600 | tf_op jit(solution)/shard_map/sir,sit->rt/dot_general | solution.py:216
  330.9 19.9 %shard_map.32 = f32[16,16,256]{2,1,0:T(8,128)} custom-call(f32[16,16,256]{2,1,0:T(8,128)} %fusion.143.x_ref), custom_call_target="tpu_custom_call" | custom-call | tf_op jit(solution)/shard_map/pallas_call | solution.py:88
  354.1 3.1 fusion.178
  369.8 24.8 %collective-permute-done.10 = bf16[4,1,1,8,96,256]{5,4,3,0,2,1:T(8,128)(2,1)S(1)} collective-permute-done((bf16[4,1,1,8,96,256]{5,4,3,0,2,1:T(8,128)(2,1)S(1)}, bf16[4,1,1,8,96,256]{5,4,3,0,2,1:T(8,128)(2,1)S(1)}, u32[]{:S(2)}, u32[]{:S(2)}) %collective-permute-start.10) | collective-permute-done | bytes 1572896 | tf_op jit(solution)/shard_map/ppermute | solution.py:176
  401.5 26.9 %collective-permute-done.11 = bf16[4,1,1,8,96,256]{5,4,3,0,2,1:T(8,128)(2,1)S(1)} collective-permute-done((bf16[4,1,1,8,96,256]{5,4,3,0,2,1:T(8,128)(2,1)S(1)}, bf16[4,1,1,8,96,256]{5,4,3,0,2,1:T(8,128)(2,1)S(1)}, u32[]{:S(2)}, u32[]{:S(2)}) %collective-permute-start.11) | collective-permute-done | bytes 1572896 | tf_op jit(solution)/shard_map/ppermute | solution.py:181
  428.3 8.7 %subtract_convert_fusion = (bf16[4,1,1,8,96,256]{5,4,3,0,2,1:T(8,128)(2,1)}, bf16[4,1,1,8,96,256]{5,4,3,0,2,1:T(8,128)(2,1)S(1)}) fusion(bf16[4,1,1,8,96,256]{5,4,3,0,2,1:T(8,128)(2,1)S(1)} %collective-permute-done.11, bf16[9,4,1,1,8,96,96]{6,5,4,1,3,2,0:T(8,128)(2,1)S(1)} %bitcast.458, f32[4,8,256,96]{2,3,1,0:T(8,128)} %fusion.79, ...), kind=kOutput, calls=%fused_computation.42 | convolution fusion | flops 162791424 | bytes 32243712 | tf_op jit(solution)/shard_map/abcdoi,abcdir->abcdor/dot_general | solution.py:169
  440.3 21.0 %shard_map.33 = f32[16,16,256]{2,1,0:T(8,128)} custom-call(f32[16,16,256]{2,1,0:T(8,128)} %bitcast.483), custom_call_target="tpu_custom_call" | custom-call | tf_op jit(solution)/shard_map/pallas_call | solution.py:88
  461.3 41.1 %shard_map.34 = f32[256,256]{1,0:T(8,128)} custom-call(f32[256,256]{1,0:T(8,128)} %bitcast.476), custom_call_target="tpu_custom_call" | custom-call | flops 1500000000 | bytes 1048576 | tf_op jit(solution)/shard_map/pallas_call | solution.py:147
  504.9 6.2 %fusion.27 = f32[4,1,1,8,96,256]{5,4,3,2,1,0:T(8,128)} fusion(f32[256,4,8,96]{0,3,2,1:T(8,128)S(1)} %copy-done.2, f32[256,256,1,1]{1,0,3,2:T(8,128)S(1)} %fusion.135, f32[4,1,1,8,96,256]{5,4,3,0,2,1:T(8,128)} %get-tuple-element.26), kind=kOutput, calls=%fused_computation.41 | convolution fusion | flops 2416705536 | bytes 9699328 | tf_op jit(solution)/shard_map/abcdir,rt->abcdit/dot_general | solution.py:226
  (124 shorter events, 65.4 us)
Async XLA Ops:
  0.0 10.2 %copy-start = (bf16[4,1,1,8,96,256]{5,4,3,2,1,0:T(8,128)(2,1)S(1)}, bf16[4,1,1,8,96,256]{5,4,3,2,1,0:T(8,128)(2,1)}, u32[]{:S(2)}) copy-start(bf16[4,1,1,8,96,256]{5,4,3,2,1,0:T(8,128)(2,1)} %param.2) | copy-start | bytes 4718596
  0.0 137.6 %collective-permute-start.1 = (bf16[4,1,1,8,96,256]{5,4,3,0,2,1:T(8,128)(2,1)}, bf16[4,1,1,8,96,256]{5,4,3,0,2,1:T(8,128)(2,1)}, u32[]{:S(2)}, u32[]{:S(2)}) collective-permute-start(bf16[4,1,1,8,96,256]{5,4,3,0,2,1:T(8,128)(2,1)} %bitcast.422), channel_id=1, source_target_pairs={{0,4},{4,8},{8,12},{12,0},{1,5},{5,9},{9,13},{13,1},{2,6},{6,10},{... | collective-permute-start | bytes 4718600 | tf_op jit(solution)/shard_map/ppermute | solution.py:181
  0.5 141.3 %collective-permute-start = (bf16[4,1,1,8,96,256]{5,4,3,0,2,1:T(8,128)(2,1)}, bf16[4,1,1,8,96,256]{5,4,3,0,2,1:T(8,128)(2,1)}, u32[]{:S(2)}, u32[]{:S(2)}) collective-permute-start(bf16[4,1,1,8,96,256]{5,4,3,0,2,1:T(8,128)(2,1)} %bitcast.423), channel_id=1, source_target_pairs={{4,0},{8,4},{12,8},{0,12},{5,1},{9,5},{13,9},{1,13},{6,2},{10,6},{... | collective-permute-start | bytes 4718600 | tf_op jit(solution)/shard_map/ppermute | solution.py:176
  2.5 143.3 %collective-permute-start.2 = (bf16[4,1,1,8,96,256]{5,4,3,0,2,1:T(8,128)(2,1)}, bf16[4,1,1,8,96,256]{5,4,3,0,2,1:T(8,128)(2,1)}, u32[]{:S(2)}, u32[]{:S(2)}) collective-permute-start(bf16[4,1,1,8,96,256]{5,4,3,0,2,1:T(8,128)(2,1)} %bitcast.424), channel_id=1, source_target_pairs={{1,0},{2,1},{3,2},{0,3},{5,4},{6,5},{7,6},{4,7},{9,8},{10,9},{11,1... | collective-permute-start | bytes 4718600 | tf_op jit(solution)/shard_map/ppermute | solution.py:176
  6.8 143.0 %collective-permute-start.3 = (bf16[4,1,1,8,96,256]{5,4,3,0,2,1:T(8,128)(2,1)}, bf16[4,1,1,8,96,256]{5,4,3,0,2,1:T(8,128)(2,1)}, u32[]{:S(2)}, u32[]{:S(2)}) collective-permute-start(bf16[4,1,1,8,96,256]{5,4,3,0,2,1:T(8,128)(2,1)} %bitcast.425), channel_id=1, source_target_pairs={{0,1},{1,2},{2,3},{3,0},{4,5},{5,6},{6,7},{7,4},{8,9},{9,10},{10,1... | collective-permute-start | bytes 4718600 | tf_op jit(solution)/shard_map/ppermute | solution.py:181
  19.7 4.3 copy-start.14
  19.7 4.3 copy-start.19
  27.4 3.5 copy-start.12
  137.6 12.2 %copy-start.6 = (f32[4,8,256,96]{2,3,1,0:T(8,128)S(1)}, f32[4,8,256,96]{2,3,1,0:T(8,128)}, u32[]{:S(2)}) copy-start(f32[4,8,256,96]{2,3,1,0:T(8,128)} %fusion.51) | copy-start | bytes 9437188
  141.8 8.1 %copy-start.4 = (f32[4,8,256,96]{2,3,1,0:T(8,128)S(1)}, f32[4,8,256,96]{2,3,1,0:T(8,128)}, u32[]{:S(2)}) copy-start(f32[4,8,256,96]{2,3,1,0:T(8,128)} %fusion.45) | copy-start | bytes 9437188
  141.8 8.1 %copy-start.5 = (f32[4,8,256,96]{2,3,1,0:T(8,128)S(1)}, f32[4,8,256,96]{2,3,1,0:T(8,128)}, u32[]{:S(2)}) copy-start(f32[4,8,256,96]{2,3,1,0:T(8,128)} %fusion.48) | copy-start | bytes 9437188
  145.8 4.1 copy-start.3
  182.7 41.0 %copy-start.15 = (f32[16,16,256]{2,1,0:T(8,128)S(1)}, f32[16,16,256]{2,1,0:T(8,128)}, u32[]{:S(2)}) copy-start(f32[16,16,256]{2,1,0:T(8,128)} %shard_map.28) | copy-start | bytes 786436
  238.3 7.4 %copy-start.11 = (bf16[4,8,96,256]{3,2,1,0:T(8,128)(2,1)S(1)}, bf16[4,8,96,256]{3,2,1,0:T(8,128)(2,1)}, u32[]{:S(2)}) copy-start(bf16[4,8,96,256]{3,2,1,0:T(8,128)(2,1)} %fusion.111) | copy-start | bytes 4718596
  238.4 35.5 %collective-permute-start.4 = (bf16[4,1,1,8,96,256]{5,4,3,0,2,1:T(8,128)(2,1)S(1)}, bf16[4,1,1,8,96,256]{5,4,3,0,2,1:T(8,128)(2,1)S(1)}, u32[]{:S(2)}, u32[]{:S(2)}) collective-permute-start(bf16[4,1,1,8,96,256]{5,4,3,0,2,1:T(8,128)(2,1)S(1)} %fusion.123), channel_id=1, source_target_pairs={{0,4},{4,8},{8,12},{12,0},{1,5},{5,9},{9,13},{13,1},{2,6},{6,10},{... | collective-permute-start | bytes 4718600 | tf_op jit(solution)/shard_map/ppermute | solution.py:181
  238.4 35.5 %collective-permute-start.5 = (bf16[4,1,1,8,96,256]{5,4,3,0,2,1:T(8,128)(2,1)S(1)}, bf16[4,1,1,8,96,256]{5,4,3,0,2,1:T(8,128)(2,1)S(1)}, u32[]{:S(2)}, u32[]{:S(2)}) collective-permute-start(bf16[4,1,1,8,96,256]{5,4,3,0,2,1:T(8,128)(2,1)S(1)} %fusion.126), channel_id=1, source_target_pairs={{4,0},{8,4},{12,8},{0,12},{5,1},{9,5},{13,9},{1,13},{6,2},{10,6},{... | collective-permute-start | bytes 4718600 | tf_op jit(solution)/shard_map/ppermute | solution.py:176
  240.1 39.1 %collective-permute-start.6 = (bf16[4,1,1,8,96,256]{5,4,3,0,2,1:T(8,128)(2,1)S(1)}, bf16[4,1,1,8,96,256]{5,4,3,0,2,1:T(8,128)(2,1)S(1)}, u32[]{:S(2)}, u32[]{:S(2)}) collective-permute-start(bf16[4,1,1,8,96,256]{5,4,3,0,2,1:T(8,128)(2,1)S(1)} %fusion.129), channel_id=1, source_target_pairs={{0,1},{1,2},{2,3},{3,0},{4,5},{5,6},{6,7},{7,4},{8,9},{9,10},{10,1... | collective-permute-start | bytes 4718600 | tf_op jit(solution)/shard_map/ppermute | solution.py:181
  240.9 69.0 %collective-permute-start.7 = (bf16[4,1,1,8,96,256]{5,4,3,0,2,1:T(8,128)(2,1)S(1)}, bf16[4,1,1,8,96,256]{5,4,3,0,2,1:T(8,128)(2,1)S(1)}, u32[]{:S(2)}, u32[]{:S(2)}) collective-permute-start(bf16[4,1,1,8,96,256]{5,4,3,0,2,1:T(8,128)(2,1)S(1)} %fusion.132), channel_id=1, source_target_pairs={{1,0},{2,1},{3,2},{0,3},{5,4},{6,5},{7,6},{4,7},{9,8},{10,9},{11,1... | collective-permute-start | bytes 4718600 | tf_op jit(solution)/shard_map/ppermute | solution.py:176
  249.1 60.9 %slice-start.2 = ((bf16[4,1,1,8,96,256]{5,4,3,0,2,1:T(8,128)(2,1)}), bf16[4,1,1,7,96,256]{5,4,3,0,2,1:T(8,128)(2,1)S(1)}, s32[]{:S(2)}) async-start(bf16[4,1,1,8,96,256]{5,4,3,0,2,1:T(8,128)(2,1)} %copy-done.9), calls=%async_computation.2 | async-start | bytes 2752512 | tf_op jit(solution)/shard_map/jit(_roll_static)/slice | solution.py:207
  249.1 60.9 %slice-start.3 = ((bf16[4,1,1,8,96,256]{5,4,3,0,2,1:T(8,128)(2,1)}), bf16[4,1,1,1,96,256]{5,4,3,0,2,1:T(8,128)(2,1)S(1)}, s32[]{:S(2)}) async-start(bf16[4,1,1,8,96,256]{5,4,3,0,2,1:T(8,128)(2,1)} %copy-done.9), calls=%async_computation.3 | async-start | bytes 393216 | tf_op jit(solution)/shard_map/jit(_roll_static)/slice | solution.py:207
  249.1 60.9 %slice-start.4 = ((bf16[4,1,1,8,96,256]{5,4,3,0,2,1:T(8,128)(2,1)}), bf16[4,1,1,7,96,256]{5,4,3,0,2,1:T(8,128)(2,1)S(1)}, s32[]{:S(2)}) async-start(bf16[4,1,1,8,96,256]{5,4,3,0,2,1:T(8,128)(2,1)} %copy-done.10), calls=%async_computation.4 | async-start | bytes 2752512 | tf_op jit(solution)/shard_map/jit(_roll_static)/slice | solution.py:207
  249.1 60.9 %slice-start.5 = ((bf16[4,1,1,8,96,256]{5,4,3,0,2,1:T(8,128)(2,1)}), bf16[4,1,1,1,96,256]{5,4,3,0,2,1:T(8,128)(2,1)S(1)}, s32[]{:S(2)}) async-start(bf16[4,1,1,8,96,256]{5,4,3,0,2,1:T(8,128)(2,1)} %copy-done.10), calls=%async_computation.5 | async-start | bytes 393216 | tf_op jit(solution)/shard_map/jit(_roll_static)/slice | solution.py:207
  321.0 29.8 %copy-start.22 = (f32[256,256]{1,0:T(8,128)S(1)}, f32[256,256]{1,0:T(8,128)}, u32[]{:S(2)}) copy-start(f32[256,256]{1,0:T(8,128)} %shard_map.31) | copy-start | bytes 786436
  321.0 31.3 %copy-start.20 = (f32[256,256]{0,1:T(8,128)S(1)}, f32[256,256]{0,1:T(8,128)}, u32[]{:S(2)}) copy-start(f32[256,256]{0,1:T(8,128)} %copy.81) | copy-start | bytes 786436
  354.1 7.8 %slice-start = ((s8[7077888]{0:T(1024)(128)(4,1)}), s8[4194304]{0:T(1024)(128)(4,1)S(1)}, s32[]{:S(2)}) async-start(s8[7077888]{0:T(1024)(128)(4,1)} %bitcast.448), calls=%async_computation | async-start | bytes 8388608
  357.2 4.6 slice-start.1
  357.8 36.8 %collective-permute-start.10 = (bf16[4,1,1,8,96,256]{5,4,3,0,2,1:T(8,128)(2,1)S(1)}, bf16[4,1,1,8,96,256]{5,4,3,0,2,1:T(8,128)(2,1)S(1)}, u32[]{:S(2)}, u32[]{:S(2)}) collective-permute-start(bf16[4,1,1,8,96,256]{5,4,3,0,2,1:T(8,128)(2,1)S(1)} %get-tuple-element.25), channel_id=1, source_target_pairs={{1,0},{2,1},{3,2},{0,3},{5,4},{6,5},{7,6},{4,7},{9,8},{10,9},{11,1... | collective-permute-start | bytes 4718600 | tf_op jit(solution)/shard_map/ppermute | solution.py:176
  359.8 37.1 %collective-permute-start.9 = (bf16[4,1,1,8,96,256]{5,4,3,0,2,1:T(8,128)(2,1)S(1)}, bf16[4,1,1,8,96,256]{5,4,3,0,2,1:T(8,128)(2,1)S(1)}, u32[]{:S(2)}, u32[]{:S(2)}) collective-permute-start(bf16[4,1,1,8,96,256]{5,4,3,0,2,1:T(8,128)(2,1)S(1)} %get-tuple-element.25), channel_id=1, source_target_pairs={{0,4},{4,8},{8,12},{12,0},{1,5},{5,9},{9,13},{13,1},{2,6},{6,10},{... | collective-permute-start | bytes 4718600 | tf_op jit(solution)/shard_map/ppermute | solution.py:181
  359.8 39.4 %collective-permute-start.8 = (bf16[4,1,1,8,96,256]{5,4,3,0,2,1:T(8,128)(2,1)S(1)}, bf16[4,1,1,8,96,256]{5,4,3,0,2,1:T(8,128)(2,1)S(1)}, u32[]{:S(2)}, u32[]{:S(2)}) collective-permute-start(bf16[4,1,1,8,96,256]{5,4,3,0,2,1:T(8,128)(2,1)S(1)} %get-tuple-element.25), channel_id=1, source_target_pairs={{4,0},{8,4},{12,8},{0,12},{5,1},{9,5},{13,9},{1,13},{6,2},{10,6},{... | collective-permute-start | bytes 4718600 | tf_op jit(solution)/shard_map/ppermute | solution.py:176
  361.5 66.8 %collective-permute-start.11 = (bf16[4,1,1,8,96,256]{5,4,3,0,2,1:T(8,128)(2,1)S(1)}, bf16[4,1,1,8,96,256]{5,4,3,0,2,1:T(8,128)(2,1)S(1)}, u32[]{:S(2)}, u32[]{:S(2)}) collective-permute-start(bf16[4,1,1,8,96,256]{5,4,3,0,2,1:T(8,128)(2,1)S(1)} %get-tuple-element.25), channel_id=1, source_target_pairs={{0,1},{1,2},{2,3},{3,0},{4,5},{5,6},{6,7},{7,4},{8,9},{9,10},{10,1... | collective-permute-start | bytes 4718600 | tf_op jit(solution)/shard_map/ppermute | solution.py:181
  461.3 41.2 %copy-start.17 = (f32[16,16,256]{2,1,0:T(8,128)S(1)}, f32[16,16,256]{2,1,0:T(8,128)}, u32[]{:S(2)}) copy-start(f32[16,16,256]{2,1,0:T(8,128)} %shard_map.33) | copy-start | bytes 786436
  461.3 41.3 %copy-start.7 = (f32[16,16,256]{2,1,0:T(8,128)S(1)}, f32[16,16,256]{2,1,0:T(8,128)}, u32[]{:S(2)}) copy-start(f32[16,16,256]{2,1,0:T(8,128)} %shard_map.32) | copy-start | bytes 786436
  (11 other events, 23.7 us)

commit v2 on v1

--- a/solution.py
+++ b/solution.py
@@ -7,7 +7,7 @@
 from jax.experimental.pallas import tpu as pltpu
 from jax.sharding import PartitionSpec as P
 
-ITERS = 2
+
 mass_term = 2.0
 MESH = pl.DeviceIdType.MESH
 HI = lax.Precision.HIGHEST
@@ -78,7 +78,7 @@
         second(off).wait_send()
 
 
-def all_sum(matrix):
+def all_sum(matrix, number=0):
     n_ta, n_xy = lax.axis_size("ta"), lax.axis_size("xy")
     n = n_ta * n_xy
     rows, cols = matrix.shape
@@ -92,19 +92,28 @@
         out_specs=pl.BlockSpec(memory_space=pltpu.VMEM),
         scratch_shapes=[pltpu.VMEM(shape, f32), pltpu.VMEM(shape, f32)]
         + [pltpu.SemaphoreType.DMA((n,))] * 4,
-        compiler_params=pltpu.CompilerParams(collective_id=0, has_side_effects=True),
+        cost_estimate=pl.CostEstimate(flops=0, bytes_accessed=64 << 20, transcendentals=0),
+        compiler_params=pltpu.CompilerParams(collective_id=number, has_side_effects=True),
     )(padded.reshape(shape))
     return out.reshape(n * per, cols)[:rows]
 
 
-def inverse_kernel(a_ref, x_ref, s_ref):
-    n = a_ref.shape[0]
-    dot = functools.partial(jnp.dot, precision=HI, preferred_element_type=f32)
+dot = functools.partial(jnp.dot, precision=HI, preferred_element_type=f32)
+
+
+def dot_t(a, b):
+    return lax.dot_general(a, b, (((0,), (0,)), ((), ())), precision=HI, preferred_element_type=f32)
+
+
+def symmetric(a):
+    return 0.5 * (a + a.T)
+
+
+def invert(a, x_ref, s_ref):
+    n = a.shape[0]
     row = lax.broadcasted_iota(jnp.int32, (n, n), 0)
     col = lax.broadcasted_iota(jnp.int32, (n, n), 1)
     eye = jnp.where(row == col, 1.0, 0.0).astype(f32)
-    a = a_ref[...]
-    a = 0.5 * (a + a.T)
     diag = a * eye
     down = lax.rsqrt(jnp.sum(diag, axis=1, keepdims=True))
     across = lax.rsqrt(jnp.sum(diag, axis=0, keepdims=True))
@@ -116,8 +125,7 @@
         power = dot(power, power)
         x = x + dot(x, power)
     x_ref[...] = x
-    left = eye - dot(a, x)
-    worst = jnp.max(jnp.abs(left))
+    worst = jnp.max(jnp.abs(eye - dot(a, x)))
 
     @pl.when(jnp.logical_not(worst < 1e-3))
     def _():
@@ -139,29 +147,48 @@
 
     x = x_ref[...]
     x = x + dot(x, eye - dot(s_ref[...], x))
-    x_ref[...] = x * down * across
-
-
-def spd_inverse(matrix):
+    return x * down * across
+
+
+def solved(a, inverse, right):
+    out = dot(inverse, right)
+    return out + dot(inverse, right - dot(a, out))
+
+
+def energy_kernel(energy_ref, o_ref, x_ref, s_ref):
+    o_ref[...] = invert(symmetric(energy_ref[...]), x_ref, s_ref)
+
+
+def alpha_kernel(curvature_ref, energy_ref, o_ref, x_ref, s_ref):
+    curvature = symmetric(curvature_ref[...])
+    inverse = invert(curvature, x_ref, s_ref)
+    o_ref[...] = solved(curvature, inverse, energy_ref[...])
+
+
+def closing_kernel(energy_ref, inverse_ref, curvature_ref, alpha_ref, fresh_ref, square_ref,
+                   gamma_ref, alpha2_ref, x_ref, s_ref):
+    fresh = fresh_ref[...]
+    beta = solved(symmetric(energy_ref[...]), inverse_ref[...], fresh)
+    second = square_ref[...] - dot_t(beta, dot(symmetric(curvature_ref[...]), beta))
+    second = symmetric(second)
+    inverse = invert(second, x_ref, s_ref)
+    alpha2 = solved(second, inverse, fresh)
+    alpha2_ref[...] = alpha2
+    gamma_ref[...] = alpha_ref[...] + dot(beta, alpha2)
+
+
+def small(kernel, count, *args):
     spec = pl.BlockSpec(memory_space=pltpu.VMEM)
-    return pl.pallas_call(
-        inverse_kernel,
-        out_shape=jax.ShapeDtypeStruct(matrix.shape, f32),
-        in_specs=[spec],
-        out_specs=spec,
-        scratch_shapes=[pltpu.VMEM(matrix.shape, f32)],
-        cost_estimate=pl.CostEstimate(flops=int(1.5e9), bytes_accessed=1 << 20, transcendentals=0),
-    )(matrix)
-
-
-def mm(a, b):
-    return jnp.dot(a, b, precision=HI)
-
-
-def solve(matrix, inverse, right):
-    out = mm(inverse, right)
-    sym = 0.5 * (matrix + matrix.T)
-    return out + mm(inverse, right - mm(sym, out))
+    shape = args[0].shape
+    out = pl.pallas_call(
+        kernel,
+        out_shape=[jax.ShapeDtypeStruct(shape, f32)] * count,
+        in_specs=[spec] * len(args),
+        out_specs=[spec] * count,
+        scratch_shapes=[pltpu.VMEM(shape, f32)] * 2,
+        cost_estimate=pl.CostEstimate(flops=int(4e9), bytes_accessed=1 << 20, transcendentals=0),
+    )(*args)
+    return out if count > 1 else out[0]
 
 
 def link_product(link_field, vector, flipped):
@@ -188,32 +215,38 @@
 LOCAL = ((0, 1), (0, -1), (3, 1), (3, -1))
 
 
-def apply_forward(rounded, links):
-    far = [shifted(rounded, *hop) for hop in HOPS]
+def neighbours(vector):
+    return [shifted(vector, *hop) for hop in HOPS]
+
+
+def far_products(far, links):
+    total = link_product(links[1], far[0], False)
+    for number in range(1, 4):
+        total = total + link_product(links[number + 1], far[number], False)
+    return total
+
+
+def near_products(rounded, links):
     total = mass_term * rounded.astype(f32) + link_product(links[0], rounded, False)
     for number, (dim, step) in enumerate(LOCAL):
         total = total + link_product(links[number + 5], jnp.roll(rounded, -step, dim), False)
-    for number in range(4):
-        total = total + link_product(links[number + 1], far[number], False)
     return total
 
 
-def apply_adjoint(image, links):
-    sent = [link_product(links[number + 1], image, True).astype(bf16) for number in range(4)]
-    far = [shifted(sent[number], axis, dim, -step) for number, (axis, dim, step) in enumerate(HOPS)]
+def sent_adjoint(image, links):
+    return [link_product(links[number + 1], image, True).astype(bf16) for number in range(4)]
+
+
+def near_adjoint(image, links):
     total = mass_term * image.astype(f32) + link_product(links[0], image, True)
     for number, (dim, step) in enumerate(LOCAL):
         term = link_product(links[number + 5], image, True).astype(bf16)
         total = total + jnp.roll(term, step, dim).astype(f32)
-    return total, far
-
-
-def rows_of(vector):
-    return vector.reshape((-1,) + vector.shape[-2:])
+    return total
 
 
 def gram(left, right, precision=None):
-    return jnp.einsum("sir,sit->rt", rows_of(left), rows_of(right), precision=precision,
+    return jnp.einsum("abcdir,abcdit->rt", left, right, precision=precision,
                       preferred_element_type=f32)
 
 
@@ -223,36 +256,42 @@
 
 
 def combine(vector, coefficients):
-    return jnp.einsum("abcdir,rt->abcdit", vector, coefficients, precision=HI,
+    return jnp.einsum("abcdir,rt->abcdit", vector, coefficients, precision=lax.Precision.HIGH,
                       preferred_element_type=f32)
 
 
 def body(sources, links):
-    residual = sources.astype(f32)
+    wide = sources.astype(f32)
+    far = neighbours(sources)
+    near = near_products(sources, links)
     energy = all_sum(gram(sources, sources))
-    energy_inv = spd_inverse(energy)
-    search = residual
-    solution = None
-    for iteration in range(ITERS):
-        rounded = search.astype(bf16)
-        full = apply_forward(rounded, links)
-        image = full.astype(bf16)
-        last = iteration + 1 == ITERS
-        if not last:
-            partial, far = apply_adjoint(image, links)
-        curvature = all_sum(image_gram(full, image))
-        alpha = solve(curvature, spd_inverse(curvature), energy)
-        step = combine(search, alpha)
-        solution = step if solution is None else solution + step
-        if not last:
-            for term in far:
-                partial = partial + term.astype(f32)
-            residual = residual - combine(partial, alpha)
-            fresh = all_sum(gram(residual, residual, HI))
-            beta = solve(energy, energy_inv, fresh)
-            search = residual + combine(search, beta)
-            energy = fresh
-    return solution
+    energy_inv = small(energy_kernel, 1, energy)
+    full = near + far_products(far, links)
+    image = full.astype(bf16)
+
+    sent = sent_adjoint(image, links)
+    full, image, *sent = lax.optimization_barrier((full, image, *sent))
+    came = []
+    for k, (axis, dim, step) in enumerate(HOPS):
+        came.append(shifted(sent[k], axis, dim, -step))
+    curvature = all_sum(image_gram(full, image))
+    alpha = small(alpha_kernel, 1, curvature, energy)
+    normal = near_adjoint(image, links)
+    for term in came:
+        normal = normal + term.astype(f32)
+
+    normal, rounded = lax.optimization_barrier((normal, normal.astype(bf16)))
+    far = neighbours(rounded)
+    residual = wide - combine(normal, alpha)
+    fresh = gram(residual, residual, lax.Precision.HIGH)
+    near = mass_term * (normal - rounded.astype(f32)) + near_products(rounded, links)
+    full, normal = lax.optimization_barrier((full, near))
+    descent = (full - combine(normal + far_products(far, links), alpha)).astype(bf16)
+    square = gram(descent, descent)
+    both = all_sum(jnp.concatenate([fresh, square], axis=0), 1)
+    size = fresh.shape[0]
+    gamma, alpha2 = small(closing_kernel, 2, energy, energy_inv, curvature, alpha, both[:size], both[size:])
+    return combine(wide, gamma) + combine(residual, alpha2)
 
 
 def solution(mesh):

time: 518 us -> 475 us (0.917)
  waiting for transfers between devices: 111 us -> 53.1 us
  Pallas kernels: 239 us -> 292 us
  matrix products: 121 us -> 87.2 us
  local copies, waits for them, and re-layouts: 23.1 us -> 16.3 us
    pallas_call x4 -> x3, Pallas kernels: 116 us -> 166 us  [all_sum(): pl.pallas_call(functools.partial(sum_kernel, n_ta, n_xy), out_shape=jax.S...]
    ppermute x6, waiting for transfers between devices: 55.1 us -> 23.1 us  [shifted(): lax.ppermute(edge, axis, [(i, (i + 1) % count) for i in range(count)])]
    dot_general x19 -> x9, matrix products: 44.3 us -> 16.7 us  [the longest x4 9.28 us: combine(): jnp.einsum('abcdir,rt->abcdit', vector, coefficients, precision=lax.Preci...]
    ppermute x6, waiting for transfers between devices: 55.5 us -> 30 us  [shifted(): lax.ppermute(edge, axis, [((i + 1) % count, i) for i in range(count)])]
    reshape x5 -> x0, local copies, waits for them, and re-layouts: 12.1 us -> none  [the longest x2 9.4 us: rows_of(): return vector.reshape((-1,) + vector.shape[-2:])]
    dot_general x27, matrix products: 76.6 us -> 70.5 us  [link_product(): jnp.einsum(einsum_form, link_field, vector, preferred_element_type=f32)]
    slice x16 -> x15, local copies, waits for them, and re-layouts: 6.29 us -> 10.6 us  [the longest x8 6.27 us: near_products(): jnp.roll(rounded, -step, dim)]
  transfers between devices with their start and end apart: 12 -> 12, of which waited for: 5 -> 2; matrix products, arithmetic and copies ran while one was open for 13% -> 14% of each run, Pallas kernels for 19% -> 46%
where the time goes in v2:
time: 475 us; the launch traced here: 468 us
  Pallas kernels  292 us (61%)
  matrix products  87.2 us (18%)
  waiting for transfers between devices  53.1 us (11%)
  starting transfers between devices  17.9 us (4%)
  local copies, waits for them, and re-layouts  16.3 us (3%)
    pallas_call x3, Pallas kernels, all_sum(): pl.pallas_call(functools.partial(sum_kernel, n_ta, n_xy), out_shape=jax.S...  166 us
    pallas_call x3, Pallas kernels, small(): pl.pallas_call(kernel, out_shape=[jax.ShapeDtypeStruct(shape, f32)] * cou...  126 us
    dot_general x27, matrix products, link_product(): jnp.einsum(einsum_form, link_field, vector, preferred_element_type=f32)  70.5 us
    ppermute x6, waiting for transfers between devices, shifted(): lax.ppermute(edge, axis, [((i + 1) % count, i) for i in range(count)])  30 us
    ppermute x6, waiting for transfers between devices, shifted(): lax.ppermute(edge, axis, [(i, (i + 1) % count) for i in range(count)])  23.1 us
    ppermute x6, starting transfers between devices, shifted(): lax.ppermute(edge, axis, [((i + 1) % count, i) for i in range(count)])  16.3 us
  transfers between devices with their start and end apart: 12, of which 2 were waited for; matrix products, arithmetic and copies ran while one was open for 14% of the time, Pallas kernels for 46%

profile of v2, /device:TPU:0, one launch (start us, length us, event | category | flops | bytes accessed | tf_op | source)
XLA Modules:
  0.0 468.4 jit_solution(2315722584255777610)
XLA Ops:
  0.0 2.4 collective-permute-start
  2.4 3.6 collective-permute-start.2
  6.0 3.3 fusion.171
  11.6 3.0 copy.37
  14.6 3.5 fusion.102
  18.1 2.1 fusion.143.x_ref
  20.2 3.4 fusion.46
  23.7 3.5 fusion.49
  27.2 3.4 fusion.52
  30.6 3.4 fusion.55
  34.0 55.3 %shard_map.28 = f32[16,16,256]{2,1,0:T(8,128)} custom-call(f32[16,16,256]{2,1,0:T(8,128)} %fusion.143.x_ref), custom_call_target="tpu_custom_call" | custom-call | bytes 67108864 | tf_op jit(solution)/shard_map/pallas_call | solution.py:88
  89.3 40.0 %shard_map.29.inverse_ref = f32[256,256]{1,0:T(8,128)} custom-call(f32[256,256]{1,0:T(8,128)} %bitcast.424), custom_call_target="tpu_custom_call" | custom-call | flops 4000000000 | bytes 1048576 | tf_op jit(solution)/shard_map/pallas_call | solution.py:183
  129.3 4.0 fusion.100
  133.4 4.0 fusion.96
  137.4 4.1 fusion.98
  141.5 8.0 %fusion.176 = (bf16[4,1,1,8,96,256]{5,4,3,0,2,1:T(8,128)(2,1)S(1)}, f32[4,1,1,8,96,256]{5,4,3,0,2,1:T(8,128)S(1)}) fusion(bf16[4,1,1,8,96,256]{5,4,3,0,2,1:T(8,128)(2,1)} %collective-permute-done.3, bf16[9,4,1,1,8,96,96]{6,5,4,1,3,2,0:T(8,128)(2,1)S(1)} %bitcast.404, f32[4,8,96,256]{3,2,1,0:T(8,128)} %fusion.96, f32[4,8,96,256]{3,2,1,0:T(8,128)} %fusion.100, ...), kind=kOutput, calls=%fused_computation.174 | convolution fusion | flops 160432128 | bytes 33816576 | tf_op jit(solution)/shard_map/abcdoi,abcdir->abcdor/dot_general | solution.py:196
  149.6 2.1 fusion.105
  163.9 3.6 collective-permute-start.7
  168.9 78.1 %shard_map.30 = f32[16,16,256]{2,1,0:T(8,128)} custom-call(f32[16,16,256]{2,1,0:T(8,128)} %bitcast.423), custom_call_target="tpu_custom_call" | custom-call | bytes 67108864 | tf_op jit(solution)/shard_map/pallas_call | solution.py:88
  253.1 41.5 %shard_map.31.alpha_ref = f32[256,256]{1,0:T(8,128)} custom-call(f32[256,256]{1,0:T(8,128)} %bitcast.427, f32[256,256]{1,0:T(8,128)} %bitcast.425), custom_call_target="tpu_custom_call" | custom-call | flops 4000000000 | bytes 1048576 | tf_op jit(solution)/shard_map/pallas_call | solution.py:183
  294.7 6.0 %fusion.177 = (bf16[4,1,1,8,96,256]{5,4,3,0,2,1:T(8,128)(2,1)S(1)}, f32[4,1,1,8,96,256]{5,4,3,0,2,1:T(8,128)S(1)}) fusion(bf16[4,1,1,8,96,256]{5,4,3,0,2,1:T(8,128)(2,1)} %collective-permute-done.7, bf16[4,1,1,8,96,256]{5,4,3,0,2,1:T(8,128)(2,1)} %collective-permute-done.6, bf16[4,1,1,8,96,256]{5,4,3,0,2,1:T(8,128)(2,1)} %collective-permute-done.5, ...), kind=kOutput, calls=%fused_computation.175 | convolution fusion | flops 169869312 | bytes 21233664 | tf_op jit(solution)/shard_map/abcdio,abcdir->abcdor/dot_general | solution.py:196
  301.4 2.1 fusion.78
  304.2 3.1 collective-permute-start.10
  310.4 2.2 fusion.64
  312.6 3.0 fusion.18
  317.0 2.6 fusion.129
  319.6 23.1 %collective-permute-done.11 = bf16[4,1,1,8,96,256]{5,4,3,0,2,1:T(8,128)(2,1)} collective-permute-done((bf16[4,1,1,8,96,256]{5,4,3,0,2,1:T(8,128)(2,1)S(1)}, bf16[4,1,1,8,96,256]{5,4,3,0,2,1:T(8,128)(2,1)}, u32[]{:S(2)}, u32[]{:S(2)}) %collective-permute-start.11) | collective-permute-done | bytes 1572896 | tf_op jit(solution)/shard_map/ppermute | solution.py:208
  344.7 30.0 %collective-permute-done.10 = bf16[4,1,1,8,96,256]{5,4,3,0,2,1:T(8,128)(2,1)} collective-permute-done((bf16[4,1,1,8,96,256]{5,4,3,0,2,1:T(8,128)(2,1)S(1)}, bf16[4,1,1,8,96,256]{5,4,3,0,2,1:T(8,128)(2,1)}, u32[]{:S(2)}, u32[]{:S(2)}) %collective-permute-start.10) | collective-permute-done | bytes 1572896 | tf_op jit(solution)/shard_map/ppermute | solution.py:203
  382.6 32.5 %shard_map.32 = f32[16,32,256]{2,1,0:T(8,128)} custom-call(f32[16,32,256]{2,1,0:T(8,128)} %bitcast.422), custom_call_target="tpu_custom_call" | custom-call | bytes 67108864 | tf_op jit(solution)/shard_map/pallas_call | solution.py:88
  417.0 45.0 %shard_map.33 = (f32[256,256]{1,0:T(8,128)}, f32[256,256]{1,0:T(8,128)}) custom-call(f32[256,256]{1,0:T(8,128)} %bitcast.426, f32[256,256]{1,0:T(8,128)} %shard_map.29.inverse_ref, f32[256,256]{1,0:T(8,128)} %bitcast.428, f32[256,256]{1,0:T(8,128)} %shard_map.31.alpha_ref, f32[256,256]{1,0:T(8,128)} %bitcast.430, f32[256,256]{1,0:T(8,128)} %bitcast.429), custom_call_target="tpu_custom_call" | custom-call | flops 4000000000 | bytes 1048576 | tf_op jit(solution)/shard_map/pallas_call | solution.py:183
  462.0 3.4 fusion.34
  465.4 2.7 fusion.27
  (93 shorter events, 39.6 us)
Async XLA Ops:
  0.0 9.4 %copy-start = (bf16[4,1,1,8,96,256]{5,4,3,2,1,0:T(8,128)(2,1)S(1)}, bf16[4,1,1,8,96,256]{5,4,3,2,1,0:T(8,128)(2,1)}, u32[]{:S(2)}) copy-start(bf16[4,1,1,8,96,256]{5,4,3,2,1,0:T(8,128)(2,1)} %param.2) | copy-start | bytes 4718596
  0.0 129.3 %collective-permute-start = (bf16[4,1,1,8,96,256]{5,4,3,0,2,1:T(8,128)(2,1)}, bf16[4,1,1,8,96,256]{5,4,3,0,2,1:T(8,128)(2,1)}, u32[]{:S(2)}, u32[]{:S(2)}) collective-permute-start(bf16[4,1,1,8,96,256]{5,4,3,0,2,1:T(8,128)(2,1)} %bitcast.382), channel_id=1, source_target_pairs={{4,0},{8,4},{12,8},{0,12},{5,1},{9,5},{13,9},{1,13},{6,2},{10,6},{... | collective-permute-start | bytes 4718600 | tf_op jit(solution)/shard_map/ppermute | solution.py:203
  2.4 130.9 %collective-permute-start.2 = (bf16[4,1,1,8,96,256]{5,4,3,0,2,1:T(8,128)(2,1)}, bf16[4,1,1,8,96,256]{5,4,3,0,2,1:T(8,128)(2,1)}, u32[]{:S(2)}, u32[]{:S(2)}) collective-permute-start(bf16[4,1,1,8,96,256]{5,4,3,0,2,1:T(8,128)(2,1)} %bitcast.383), channel_id=1, source_target_pairs={{1,0},{2,1},{3,2},{0,3},{5,4},{6,5},{7,6},{4,7},{9,8},{10,9},{11,1... | collective-permute-start | bytes 4718600 | tf_op jit(solution)/shard_map/ppermute | solution.py:203
  6.0 131.3 %collective-permute-start.1 = (bf16[4,1,1,8,96,256]{5,4,3,0,2,1:T(8,128)(2,1)}, bf16[4,1,1,8,96,256]{5,4,3,0,2,1:T(8,128)(2,1)}, u32[]{:S(2)}, u32[]{:S(2)}) collective-permute-start(bf16[4,1,1,8,96,256]{5,4,3,0,2,1:T(8,128)(2,1)} %bitcast.384), channel_id=1, source_target_pairs={{0,4},{4,8},{8,12},{12,0},{1,5},{5,9},{9,13},{13,1},{2,6},{6,10},{... | collective-permute-start | bytes 4718600 | tf_op jit(solution)/shard_map/ppermute | solution.py:208
  6.0 135.4 %collective-permute-start.3 = (bf16[4,1,1,8,96,256]{5,4,3,0,2,1:T(8,128)(2,1)}, bf16[4,1,1,8,96,256]{5,4,3,0,2,1:T(8,128)(2,1)}, u32[]{:S(2)}, u32[]{:S(2)}) collective-permute-start(bf16[4,1,1,8,96,256]{5,4,3,0,2,1:T(8,128)(2,1)} %bitcast.385), channel_id=1, source_target_pairs={{0,1},{1,2},{2,3},{3,0},{4,5},{5,6},{6,7},{7,4},{8,9},{9,10},{10,1... | collective-permute-start | bytes 4718600 | tf_op jit(solution)/shard_map/ppermute | solution.py:208
  14.6 3.5 copy-start.11
  18.1 2.1 copy-start.10
  18.1 2.1 copy-start.12
  20.2 3.4 copy-start.9
  23.7 3.5 copy-start.8
  129.3 12.1 %slice-start = ((s8[7077888]{0:T(1024)(128)(4,1)}), s8[4194304]{0:T(1024)(128)(4,1)S(1)}, s32[]{:S(2)}) async-start(s8[7077888]{0:T(1024)(128)(4,1)} %bitcast.402), calls=%async_computation | async-start | bytes 8388608
  133.3 8.1 %slice-start.1 = ((s8[7077888]{0:T(1024)(128)(4,1)}), s8[2883584]{0:T(1024)(128)(4,1)S(1)}, s32[]{:S(2)}) async-start(s8[7077888]{0:T(1024)(128)(4,1)} %bitcast.402), calls=%async_computation.1 | async-start | bytes 5767168
  133.4 8.1 %copy-start.5 = (f32[4,8,256,96]{2,3,1,0:T(8,128)S(1)}, f32[4,8,256,96]{2,3,1,0:T(8,128)}, u32[]{:S(2)}) copy-start(f32[4,8,256,96]{2,3,1,0:T(8,128)} %fusion.46) | copy-start | bytes 9437188
  137.4 4.1 copy-start.4
  149.6 17.9 %copy-start.1 = (f32[4,1,1,8,96,256]{5,4,3,0,2,1:T(8,128)}, f32[4,1,1,8,96,256]{5,4,3,0,2,1:T(8,128)S(1)}, u32[]{:S(2)}) copy-start(f32[4,1,1,8,96,256]{5,4,3,0,2,1:T(8,128)S(1)} %get-tuple-element.25) | copy-start | bytes 9437188
  157.7 1.9 copy-start.7
  158.3 3.1 copy-start.6
  161.4 133.2 %collective-permute-start.4 = (bf16[4,1,1,8,96,256]{5,4,3,0,2,1:T(8,128)(2,1)}, bf16[4,1,1,8,96,256]{5,4,3,0,2,1:T(8,128)(2,1)}, u32[]{:S(2)}, u32[]{:S(2)}) collective-permute-start(bf16[4,1,1,8,96,256]{5,4,3,0,2,1:T(8,128)(2,1)} %fusion.105), channel_id=1, source_target_pairs={{0,4},{4,8},{8,12},{12,0},{1,5},{5,9},{9,13},{13,1},{2,6},{6,10},{... | collective-permute-start | bytes 4718600 | tf_op jit(solution)/shard_map/ppermute | solution.py:208
  161.5 133.1 %collective-permute-start.5 = (bf16[4,1,1,8,96,256]{5,4,3,0,2,1:T(8,128)(2,1)}, bf16[4,1,1,8,96,256]{5,4,3,0,2,1:T(8,128)(2,1)}, u32[]{:S(2)}, u32[]{:S(2)}) collective-permute-start(bf16[4,1,1,8,96,256]{5,4,3,0,2,1:T(8,128)(2,1)} %fusion.108), channel_id=1, source_target_pairs={{4,0},{8,4},{12,8},{0,12},{5,1},{9,5},{13,9},{1,13},{6,2},{10,6},{... | collective-permute-start | bytes 4718600 | tf_op jit(solution)/shard_map/ppermute | solution.py:203
  163.2 131.4 %collective-permute-start.6 = (bf16[4,1,1,8,96,256]{5,4,3,0,2,1:T(8,128)(2,1)}, bf16[4,1,1,8,96,256]{5,4,3,0,2,1:T(8,128)(2,1)}, u32[]{:S(2)}, u32[]{:S(2)}) collective-permute-start(bf16[4,1,1,8,96,256]{5,4,3,0,2,1:T(8,128)(2,1)} %fusion.111), channel_id=1, source_target_pairs={{0,1},{1,2},{2,3},{3,0},{4,5},{5,6},{6,7},{7,4},{8,9},{9,10},{10,1... | collective-permute-start | bytes 4718600 | tf_op jit(solution)/shard_map/ppermute | solution.py:208
  163.9 130.7 %collective-permute-start.7 = (bf16[4,1,1,8,96,256]{5,4,3,0,2,1:T(8,128)(2,1)}, bf16[4,1,1,8,96,256]{5,4,3,0,2,1:T(8,128)(2,1)}, u32[]{:S(2)}, u32[]{:S(2)}) collective-permute-start(bf16[4,1,1,8,96,256]{5,4,3,0,2,1:T(8,128)(2,1)} %fusion.114), channel_id=1, source_target_pairs={{1,0},{2,1},{3,2},{0,3},{5,4},{6,5},{7,6},{4,7},{9,8},{10,9},{11,1... | collective-permute-start | bytes 4718600 | tf_op jit(solution)/shard_map/ppermute | solution.py:203
  253.1 41.5 %slice-start.4 = ((bf16[4,1,1,8,96,256]{5,4,3,0,2,1:T(8,128)(2,1)}), bf16[4,1,1,1,96,256]{5,4,3,0,2,1:T(8,128)(2,1)S(1)}, s32[]{:S(2)}) async-start(bf16[4,1,1,8,96,256]{5,4,3,0,2,1:T(8,128)(2,1)} %copy-done.6), calls=%async_computation.4 | async-start | bytes 393216 | tf_op jit(solution)/shard_map/jit(_roll_static)/slice | solution.py:244
  253.1 41.6 %slice-start.5 = ((bf16[4,1,1,8,96,256]{5,4,3,0,2,1:T(8,128)(2,1)}), bf16[4,1,1,1,96,256]{5,4,3,0,2,1:T(8,128)(2,1)S(1)}, s32[]{:S(2)}) async-start(bf16[4,1,1,8,96,256]{5,4,3,0,2,1:T(8,128)(2,1)} %copy-done.7), calls=%async_computation.5 | async-start | bytes 393216 | tf_op jit(solution)/shard_map/jit(_roll_static)/slice | solution.py:244
  300.7 8.6 %slice-start.2 = ((s8[7077888]{0:T(1024)(128)(4,1)}), s8[4194304]{0:T(1024)(128)(4,1)S(1)}, s32[]{:S(2)}) async-start(s8[7077888]{0:T(1024)(128)(4,1)} %bitcast.411), calls=%async_computation.2 | async-start | bytes 8388608
  301.0 8.2 %slice-start.3 = ((s8[7077888]{0:T(1024)(128)(4,1)}), s8[2883584]{0:T(1024)(128)(4,1)S(1)}, s32[]{:S(2)}) async-start(s8[7077888]{0:T(1024)(128)(4,1)} %bitcast.411), calls=%async_computation.3 | async-start | bytes 5767168
  303.5 39.3 %collective-permute-start.11 = (bf16[4,1,1,8,96,256]{5,4,3,0,2,1:T(8,128)(2,1)S(1)}, bf16[4,1,1,8,96,256]{5,4,3,0,2,1:T(8,128)(2,1)}, u32[]{:S(2)}, u32[]{:S(2)}) collective-permute-start(bf16[4,1,1,8,96,256]{5,4,3,0,2,1:T(8,128)(2,1)S(1)} %get-tuple-element.24), channel_id=1, source_target_pairs={{0,1},{1,2},{2,3},{3,0},{4,5},{5,6},{6,7},{7,4},{8,9},{9,10},{10,1... | collective-permute-start | bytes 4718600 | tf_op jit(solution)/shard_map/ppermute | solution.py:208
  304.2 70.5 %collective-permute-start.10 = (bf16[4,1,1,8,96,256]{5,4,3,0,2,1:T(8,128)(2,1)S(1)}, bf16[4,1,1,8,96,256]{5,4,3,0,2,1:T(8,128)(2,1)}, u32[]{:S(2)}, u32[]{:S(2)}) collective-permute-start(bf16[4,1,1,8,96,256]{5,4,3,0,2,1:T(8,128)(2,1)S(1)} %get-tuple-element.24), channel_id=1, source_target_pairs={{1,0},{2,1},{3,2},{0,3},{5,4},{6,5},{7,6},{4,7},{9,8},{10,9},{11,1... | collective-permute-start | bytes 4718600 | tf_op jit(solution)/shard_map/ppermute | solution.py:203
  307.3 69.4 %collective-permute-start.9 = (bf16[4,1,1,8,96,256]{5,4,3,0,2,1:T(8,128)(2,1)S(1)}, bf16[4,1,1,8,96,256]{5,4,3,0,2,1:T(8,128)(2,1)}, u32[]{:S(2)}, u32[]{:S(2)}) collective-permute-start(bf16[4,1,1,8,96,256]{5,4,3,0,2,1:T(8,128)(2,1)S(1)} %get-tuple-element.24), channel_id=1, source_target_pairs={{0,4},{4,8},{8,12},{12,0},{1,5},{5,9},{9,13},{13,1},{2,6},{6,10},{... | collective-permute-start | bytes 4718600 | tf_op jit(solution)/shard_map/ppermute | solution.py:208
  307.3 71.4 %collective-permute-start.8 = (bf16[4,1,1,8,96,256]{5,4,3,0,2,1:T(8,128)(2,1)S(1)}, bf16[4,1,1,8,96,256]{5,4,3,0,2,1:T(8,128)(2,1)S(1)}, u32[]{:S(2)}, u32[]{:S(2)}) collective-permute-start(bf16[4,1,1,8,96,256]{5,4,3,0,2,1:T(8,128)(2,1)S(1)} %get-tuple-element.24), channel_id=1, source_target_pairs={{4,0},{8,4},{12,8},{0,12},{5,1},{9,5},{13,9},{1,13},{6,2},{10,6},{... | collective-permute-start | bytes 4718600 | tf_op jit(solution)/shard_map/ppermute | solution.py:203
  312.6 3.0 copy-start.13
  317.0 27.7 %copy-start.3 = (f32[4,8,96,256]{3,2,1,0:T(8,128)}, f32[4,8,96,256]{3,2,1,0:T(8,128)S(1)}, u32[]{:S(2)}) copy-start(f32[4,8,96,256]{3,2,1,0:T(8,128)S(1)} %fusion.29) | copy-start | bytes 9437188
  462.0 3.4 copy-start.14
  (1 other events, 1.9 us)

commit v3 on v2

--- a/solution.py
+++ b/solution.py
@@ -78,12 +78,11 @@
         second(off).wait_send()
 
 
-def all_sum(matrix, number=0):
+def all_sum(matrix):
     n_ta, n_xy = lax.axis_size("ta"), lax.axis_size("xy")
     n = n_ta * n_xy
     rows, cols = matrix.shape
     per = -(-rows // n)
-    padded = jnp.pad(matrix, ((0, per * n - rows), (0, 0))) if per * n != rows else matrix
     shape = (n, per, cols)
     out = pl.pallas_call(
         functools.partial(sum_kernel, n_ta, n_xy),
@@ -93,9 +92,30 @@
         scratch_shapes=[pltpu.VMEM(shape, f32), pltpu.VMEM(shape, f32)]
         + [pltpu.SemaphoreType.DMA((n,))] * 4,
         cost_estimate=pl.CostEstimate(flops=0, bytes_accessed=64 << 20, transcendentals=0),
-        compiler_params=pltpu.CompilerParams(collective_id=number, has_side_effects=True),
-    )(padded.reshape(shape))
+        compiler_params=pltpu.CompilerParams(collective_id=0, has_side_effects=True),
+    )(jnp.pad(matrix, ((0, per * n - rows), (0, 0))).reshape(shape))
     return out.reshape(n * per, cols)[:rows]
+
+
+def triangle(n):
+    return lax.broadcasted_iota(jnp.int32, (n, n), 0) - lax.broadcasted_iota(jnp.int32, (n, n), 1)
+
+
+def pack(first, second):
+    n = first.shape[0]
+    where = triangle(n)
+    diag = jnp.sum(jnp.where(where == 0, second, 0.0), axis=0, keepdims=True)
+    return jnp.concatenate([jnp.where(where >= 0, first, second), diag], axis=0)
+
+
+def unpack(ref):
+    n = ref.shape[1]
+    where = triangle(n)
+    both = ref[:n, :]
+    turned = both.T
+    first = jnp.where(where >= 0, both, turned)
+    second = jnp.where(where < 0, both, turned)
+    return first, jnp.where(where == 0, ref[n:n + 1, :], second)
 
 
 dot = functools.partial(jnp.dot, precision=HI, preferred_element_type=f32)
@@ -155,22 +175,21 @@
     return out + dot(inverse, right - dot(a, out))
 
 
-def energy_kernel(energy_ref, o_ref, x_ref, s_ref):
-    o_ref[...] = invert(symmetric(energy_ref[...]), x_ref, s_ref)
-
-
-def alpha_kernel(curvature_ref, energy_ref, o_ref, x_ref, s_ref):
-    curvature = symmetric(curvature_ref[...])
+def alpha_kernel(both_ref, o_ref, x_ref, s_ref):
+    energy, curvature = unpack(both_ref)
     inverse = invert(curvature, x_ref, s_ref)
-    o_ref[...] = solved(curvature, inverse, energy_ref[...])
-
-
-def closing_kernel(energy_ref, inverse_ref, curvature_ref, alpha_ref, fresh_ref, square_ref,
-                   gamma_ref, alpha2_ref, x_ref, s_ref):
-    fresh = fresh_ref[...]
-    beta = solved(symmetric(energy_ref[...]), inverse_ref[...], fresh)
-    second = square_ref[...] - dot_t(beta, dot(symmetric(curvature_ref[...]), beta))
-    second = symmetric(second)
+    o_ref[...] = solved(curvature, inverse, energy)
+
+
+def energy_kernel(both_ref, o_ref, x_ref, s_ref):
+    o_ref[...] = invert(unpack(both_ref)[0], x_ref, s_ref)
+
+
+def closing_kernel(both_ref, inverse_ref, alpha_ref, late_ref, gamma_ref, alpha2_ref, x_ref, s_ref):
+    energy, curvature = unpack(both_ref)
+    fresh, square = unpack(late_ref)
+    beta = solved(energy, inverse_ref[...], fresh)
+    second = symmetric(square - dot_t(beta, dot(curvature, beta)))
     inverse = invert(second, x_ref, s_ref)
     alpha2 = solved(second, inverse, fresh)
     alpha2_ref[...] = alpha2
@@ -179,7 +198,7 @@
 
 def small(kernel, count, *args):
     spec = pl.BlockSpec(memory_space=pltpu.VMEM)
-    shape = args[0].shape
+    shape = (args[0].shape[1],) * 2
     out = pl.pallas_call(
         kernel,
         out_shape=[jax.ShapeDtypeStruct(shape, f32)] * count,
@@ -219,11 +238,39 @@
     return [shifted(vector, *hop) for hop in HOPS]
 
 
-def far_products(far, links):
-    total = link_product(links[1], far[0], False)
-    for number in range(1, 4):
-        total = total + link_product(links[number + 1], far[number], False)
-    return total
+def hop_products(numbers, far, links):
+    return sum(link_product(links[number + 1], far[number], False) for number in numbers)
+
+
+def fold_kernel(sites, near_ref, plus_ref, minus_ref, lp_ref, lm_ref, y_ref, image_ref, up_ref, um_ref):
+    mul = functools.partial(lax.dot_general, preferred_element_type=f32)
+    straight, turned = (((1,), (0,)), ((), ())), (((0,), (0,)), ((), ()))
+    for s in range(sites):
+        plus, minus = lp_ref[0, s], lm_ref[0, s]
+        y = near_ref[s] + mul(plus, plus_ref[s], straight) + mul(minus, minus_ref[s], straight)
+        image = y.astype(bf16)
+        y_ref[s] = y
+        image_ref[s] = image
+        up_ref[s] = mul(plus, image, turned).astype(bf16)
+        um_ref[s] = mul(minus, image, turned).astype(bf16)
+
+
+def fold(near, plus, minus, links):
+    shape = near.shape
+    total, (o, r), i = near.size // (shape[-1] * shape[-2]), shape[-2:], links.shape[-1]
+    sites = shape[3]
+    vec = pl.BlockSpec((sites, o, r), lambda g: (g, 0, 0))
+    flat = lambda v: v.reshape(total, o, r)
+    whole = links.reshape(links.shape[0], total, o, i)
+    outs = pl.pallas_call(
+        functools.partial(fold_kernel, sites),
+        grid=(total // sites,),
+        out_shape=[jax.ShapeDtypeStruct((total, o, r), d) for d in (f32, bf16, bf16, bf16)],
+        in_specs=[vec, vec, vec] + [pl.BlockSpec((1, sites, o, i), lambda g, k=k: (k, g, 0, 0)) for k in (3, 4)],
+        out_specs=[vec] * 4,
+        cost_estimate=pl.CostEstimate(flops=int(2e9), bytes_accessed=20 << 20, transcendentals=0),
+    )(flat(near), flat(plus), flat(minus), whole, whole)
+    return [v.reshape(shape) for v in outs]
 
 
 def near_products(rounded, links):
@@ -231,10 +278,6 @@
     for number, (dim, step) in enumerate(LOCAL):
         total = total + link_product(links[number + 5], jnp.roll(rounded, -step, dim), False)
     return total
-
-
-def sent_adjoint(image, links):
-    return [link_product(links[number + 1], image, True).astype(bf16) for number in range(4)]
 
 
 def near_adjoint(image, links):
@@ -263,34 +306,33 @@
 def body(sources, links):
     wide = sources.astype(f32)
     far = neighbours(sources)
-    near = near_products(sources, links)
-    energy = all_sum(gram(sources, sources))
-    energy_inv = small(energy_kernel, 1, energy)
-    full = near + far_products(far, links)
-    image = full.astype(bf16)
-
-    sent = sent_adjoint(image, links)
+    near = near_products(sources, links) + hop_products((0, 1), far, links)
+    energy = gram(sources, sources)
+    full, image, *along = fold(near, far[2], far[3], links)
+    sent = [link_product(links[k + 1], image, True).astype(bf16) for k in range(2)] + along
     full, image, *sent = lax.optimization_barrier((full, image, *sent))
     came = []
     for k, (axis, dim, step) in enumerate(HOPS):
         came.append(shifted(sent[k], axis, dim, -step))
-    curvature = all_sum(image_gram(full, image))
-    alpha = small(alpha_kernel, 1, curvature, energy)
+    early = all_sum(pack(energy, symmetric(image_gram(full, image))))
     normal = near_adjoint(image, links)
     for term in came:
         normal = normal + term.astype(f32)
 
     normal, rounded = lax.optimization_barrier((normal, normal.astype(bf16)))
-    far = neighbours(rounded)
+    far = []
+    for hop in HOPS:
+        far.append(shifted(rounded, *hop))
+    alpha = small(alpha_kernel, 1, early)
+    energy_inv = small(energy_kernel, 1, early)
     residual = wide - combine(normal, alpha)
     fresh = gram(residual, residual, lax.Precision.HIGH)
     near = mass_term * (normal - rounded.astype(f32)) + near_products(rounded, links)
     full, normal = lax.optimization_barrier((full, near))
-    descent = (full - combine(normal + far_products(far, links), alpha)).astype(bf16)
-    square = gram(descent, descent)
-    both = all_sum(jnp.concatenate([fresh, square], axis=0), 1)
-    size = fresh.shape[0]
-    gamma, alpha2 = small(closing_kernel, 2, energy, energy_inv, curvature, alpha, both[:size], both[size:])
+    normal = normal + hop_products((0, 1), far, links) + hop_products((2, 3), far, links)
+    descent = (full - combine(normal, alpha)).astype(bf16)
+    late = all_sum(pack(fresh, gram(descent, descent)))
+    gamma, alpha2 = small(closing_kernel, 2, early, energy_inv, alpha, late)
     return combine(wide, gamma) + combine(residual, alpha2)
 
 

time: 475 us -> 466 us (0.981)
  waiting for transfers between devices: 53.1 us -> 112 us
  Pallas kernels: 292 us -> 247 us
  matrix products: 87.2 us -> 61.6 us
    ppermute x6, waiting for transfers between devices: 23.1 us -> 81.9 us  [shifted(): lax.ppermute(edge, axis, [(i, (i + 1) % count) for i in range(count)])]
    pallas_call x3 -> x2, Pallas kernels: 166 us -> 113 us  [all_sum(): pl.pallas_call(functools.partial(sum_kernel, n_ta, n_xy), out_shape=jax.S...]
    dot_general x27 -> x23, matrix products: 70.5 us -> 45.3 us  [link_product(): jnp.einsum(einsum_form, link_field, vector, preferred_element_type=f32)]
    pallas_call x0 -> x1, Pallas kernels: none -> 7.57 us  [fold(): pl.pallas_call(functools.partial(fold_kernel, sites), grid=(total // site...]
  transfers between devices with their start and end apart: 12 -> 12, of which waited for: 2 -> 5; matrix products, arithmetic and copies ran while one was open for 14% -> 7% of each run, Pallas kernels for 46% -> 36%
where the time goes in v3:
time: 466 us; the launch traced here: 457 us
  Pallas kernels  247 us (53%)
  waiting for transfers between devices  112 us (24%)
  matrix products  61.6 us (13%)
  starting transfers between devices  18.7 us (4%)
  local copies, waits for them, and re-layouts  17.5 us (4%)
    pallas_call x3, Pallas kernels, small(): pl.pallas_call(kernel, out_shape=[jax.ShapeDtypeStruct(shape, f32)] * cou...  127 us
    pallas_call x2, Pallas kernels, all_sum(): pl.pallas_call(functools.partial(sum_kernel, n_ta, n_xy), out_shape=jax.S...  113 us
    ppermute x6, waiting for transfers between devices, shifted(): lax.ppermute(edge, axis, [(i, (i + 1) % count) for i in range(count)])  81.9 us
    dot_general x23, matrix products, link_product(): jnp.einsum(einsum_form, link_field, vector, preferred_element_type=f32)  45.3 us
    ppermute x6, waiting for transfers between devices, shifted(): lax.ppermute(edge, axis, [((i + 1) % count, i) for i in range(count)])  29.6 us
    ppermute x6, starting transfers between devices, shifted(): lax.ppermute(edge, axis, [((i + 1) % count, i) for i in range(count)])  15.6 us
    dot_general x4, matrix products, combine(): jnp.einsum('abcdir,rt->abcdit', vector, coefficients, precision=lax.Preci...  9.44 us
  transfers between devices with their start and end apart: 12, of which 5 were waited for; matrix products, arithmetic and copies ran while one was open for 7% of the time, Pallas kernels for 36%

profile of v3, /device:TPU:0, one launch (start us, length us, event | category | flops | bytes accessed | tf_op | source)
XLA Modules:
  0.0 456.8 jit_solution(3618521845780905526)
XLA Ops:
  0.5 2.0 collective-permute-start
  2.5 4.3 collective-permute-start.2
  6.8 1.8 fusion.155
  9.0 2.6 copy-done
  14.5 20.6 %collective-permute-done.1 = bf16[4,1,1,8,96,256]{5,4,3,0,2,1:T(8,128)(2,1)S(1)} collective-permute-done((bf16[4,1,1,8,96,256]{5,4,3,0,2,1:T(8,128)(2,1)}, bf16[4,1,1,8,96,256]{5,4,3,0,2,1:T(8,128)(2,1)S(1)}, u32[]{:S(2)}, u32[]{:S(2)}) %collective-permute-start.1) | collective-permute-done | bytes 1572896 | tf_op jit(solution)/shard_map/ppermute | solution.py:227
  35.1 2.2 fusion.84
  37.5 5.5 %fusion.5 = f32[4,1,1,8,96,256]{5,4,3,0,2,1:T(8,128)} fusion(f32[4,8,256,96]{2,3,1,0:T(8,128)S(1)} %fusion.52, f32[4,8,256,96]{2,3,1,0:T(8,128)S(1)} %fusion.49, f32[4,8,256,96]{2,3,1,0:T(8,128)S(1)} %fusion.46, f32[4,8,256,96]{2,3,1,0:T(8,128)S(1)} %fusion.43, f32[4,8,96,256]{3,2,1,0:T(8,128)S(1)} %fusion.88, f32[4,8,96,256]{3,2,1,0:T(8,128)} %fusion.84, ...), kind=kOutput, calls=%fused_computation.11 | convolution fusion | flops 158072832 | bytes 25952256 | tf_op jit(solution)/shard_map/abcdoi,abcdir->abcdor/dot_general | solution.py:215
  43.1 32.4 %collective-permute-done.3 = bf16[4,1,1,8,96,256]{5,4,3,2,1,0:T(8,128)(2,1)} collective-permute-done((bf16[4,1,1,8,96,256]{5,4,3,2,1,0:T(8,128)(2,1)}, bf16[4,1,1,8,96,256]{5,4,3,2,1,0:T(8,128)(2,1)}, u32[]{:S(2)}, u32[]{:S(2)}) %collective-permute-start.3) | collective-permute-done | bytes 1572896 | tf_op jit(solution)/shard_map/ppermute | solution.py:227
  75.5 7.6 %shard_map.28 = (f32[32,96,256]{2,1,0:T(8,128)}, bf16[32,96,256]{2,1,0:T(8,128)(2,1)}, bf16[32,96,256]{2,1,0:T(8,128)(2,1)}, bf16[32,96,256]{2,1,0:T(8,128)(2,1)}) custom-call(f32[32,96,256]{2,1,0:T(8,128)} %bitcast.404, bf16[32,96,256]{2,1,0:T(8,128)(2,1)} %bitcast.407, bf16[32,96,256]{2,1,0:T(8,128)(2,1)} %bitcast.46.minus_ref, ...), custom_call_target="tpu_custom_call" | custom-call | flops 2000000000 | bytes 20971520 | tf_op jit(solution)/shard_map/pallas_call | solution.py:265
  83.0 3.5 fusion.92
  86.5 2.9 fusion.93
  89.4 2.9 fusion.94
  94.1 2.3 fusion.103
  107.0 2.6 collective-permute-start.7
  110.4 84.8 %shard_map.29 = f32[16,17,256]{2,1,0:T(8,128)} custom-call(f32[16,17,256]{2,1,0:T(8,128)} %reshape.379.x_ref), custom_call_target="tpu_custom_call" | custom-call | bytes 67108864 | tf_op jit(solution)/shard_map/pallas_call | solution.py:87
  197.0 1.8 fusion.97
  201.3 41.6 %shard_map.31.alpha_ref = f32[256,256]{1,0:T(8,128)} custom-call(f32[257,256]{1,0:T(8,128)} %slice.181.both_ref), custom_call_target="tpu_custom_call" | custom-call | flops 4000000000 | bytes 1048576 | tf_op jit(solution)/shard_map/pallas_call | solution.py:202
  243.0 39.9 %shard_map.30.inverse_ref = f32[256,256]{1,0:T(8,128)} custom-call(f32[257,256]{1,0:T(8,128)} %slice.181.both_ref), custom_call_target="tpu_custom_call" | custom-call | flops 4000000000 | bytes 1048576 | tf_op jit(solution)/shard_map/pallas_call | solution.py:202
  282.9 8.0 %fusion.159 = (bf16[4,1,1,8,96,256]{5,4,3,0,2,1:T(8,128)(2,1)S(1)}, f32[4,1,1,8,96,256]{5,4,3,0,2,1:T(8,128)S(1)}) fusion(bf16[4,1,1,8,96,256]{5,4,3,0,2,1:T(8,128)(2,1)} %collective-permute-done.7, bf16[4,1,1,8,96,256]{5,4,3,0,2,1:T(8,128)(2,1)} %collective-permute-done.6, bf16[4,1,1,8,96,256]{5,4,3,0,2,1:T(8,128)(2,1)} %collective-permute-done.5, ...), kind=kOutput, calls=%fused_computation.170 | convolution fusion | flops 169869312 | bytes 21233664 | tf_op jit(solution)/shard_map/abcdio,abcdir->abcdor/dot_general | solution.py:215
  293.1 3.2 collective-permute-start.10
  302.7 28.9 %collective-permute-done.11 = bf16[4,1,1,8,96,256]{5,4,3,0,2,1:T(8,128)(2,1)} collective-permute-done((bf16[4,1,1,8,96,256]{5,4,3,0,2,1:T(8,128)(2,1)S(1)}, bf16[4,1,1,8,96,256]{5,4,3,0,2,1:T(8,128)(2,1)}, u32[]{:S(2)}, u32[]{:S(2)}) %collective-permute-start.11) | collective-permute-done | bytes 1572896 | tf_op jit(solution)/shard_map/ppermute | solution.py:227
  331.5 2.0 fusion.66
  333.5 29.5 %collective-permute-done.10 = bf16[4,1,1,8,96,256]{5,4,3,0,2,1:T(8,128)(2,1)} collective-permute-done((bf16[4,1,1,8,96,256]{5,4,3,0,2,1:T(8,128)(2,1)S(1)}, bf16[4,1,1,8,96,256]{5,4,3,0,2,1:T(8,128)(2,1)}, u32[]{:S(2)}, u32[]{:S(2)}) %collective-permute-start.10) | collective-permute-done | bytes 1572896 | tf_op jit(solution)/shard_map/ppermute | solution.py:222
  363.0 2.0 fusion.68
  365.0 2.0 fusion.70
  366.9 2.0 fusion.72
  368.9 1.9 fusion.25
  372.2 2.8 fusion.123
  375.8 27.7 %shard_map.32 = f32[16,17,256]{2,1,0:T(8,128)} custom-call(f32[16,17,256]{2,1,0:T(8,128)} %reshape.396.x_ref), custom_call_target="tpu_custom_call" | custom-call | bytes 67108864 | tf_op jit(solution)/shard_map/pallas_call | solution.py:87
  405.3 45.0 %shard_map.33 = (f32[256,256]{1,0:T(8,128)}, f32[256,256]{1,0:T(8,128)}) custom-call(f32[257,256]{1,0:T(8,128)} %slice.181.both_ref, f32[256,256]{1,0:T(8,128)} %shard_map.30.inverse_ref, f32[256,256]{1,0:T(8,128)} %shard_map.31.alpha_ref, f32[257,256]{1,0:T(8,128)} %slice.192.late_ref), custom_call_target="tpu_custom_call" | custom-call | flops 4000000000 | bytes 1048576 | tf_op jit(solution)/shard_map/pallas_call | solution.py:202
  450.4 3.4 fusion.33
  453.8 2.7 fusion.27
  (89 shorter events, 33.6 us)
Async XLA Ops:
  0.0 8.6 %copy-start.1 = (bf16[4,1,1,8,96,256]{5,4,3,2,1,0:T(8,128)(2,1)S(1)}, bf16[4,1,1,8,96,256]{5,4,3,2,1,0:T(8,128)(2,1)}, u32[]{:S(2)}) copy-start(bf16[4,1,1,8,96,256]{5,4,3,2,1,0:T(8,128)(2,1)} %param.2) | copy-start | bytes 4718596
  0.0 35.1 %collective-permute-start.1 = (bf16[4,1,1,8,96,256]{5,4,3,0,2,1:T(8,128)(2,1)}, bf16[4,1,1,8,96,256]{5,4,3,0,2,1:T(8,128)(2,1)S(1)}, u32[]{:S(2)}, u32[]{:S(2)}) collective-permute-start(bf16[4,1,1,8,96,256]{5,4,3,0,2,1:T(8,128)(2,1)} %bitcast.389), channel_id=1, source_target_pairs={{0,4},{4,8},{8,12},{12,0},{1,5},{5,9},{9,13},{13,1},{2,6},{6,10},{... | collective-permute-start | bytes 4718600 | tf_op jit(solution)/shard_map/ppermute | solution.py:227
  0.5 37.0 %collective-permute-start = (bf16[4,1,1,8,96,256]{5,4,3,0,2,1:T(8,128)(2,1)}, bf16[4,1,1,8,96,256]{5,4,3,0,2,1:T(8,128)(2,1)}, u32[]{:S(2)}, u32[]{:S(2)}) collective-permute-start(bf16[4,1,1,8,96,256]{5,4,3,0,2,1:T(8,128)(2,1)} %bitcast.390), channel_id=1, source_target_pairs={{4,0},{8,4},{12,8},{0,12},{5,1},{9,5},{13,9},{1,13},{6,2},{10,6},{... | collective-permute-start | bytes 4718600 | tf_op jit(solution)/shard_map/ppermute | solution.py:222
  2.5 40.6 %collective-permute-start.2 = (bf16[4,1,1,8,96,256]{5,4,3,2,1,0:T(8,128)(2,1)}, bf16[4,1,1,8,96,256]{5,4,3,2,1,0:T(8,128)(2,1)S(1)}, u32[]{:S(2)}, u32[]{:S(2)}) collective-permute-start(bf16[4,1,1,8,96,256]{5,4,3,2,1,0:T(8,128)(2,1)} %param.2), channel_id=1, source_target_pairs={{1,0},{2,1},{3,2},{0,3},{5,4},{6,5},{7,6},{4,7},{9,8},{10,9},{11,1... | collective-permute-start | bytes 4718600 | tf_op jit(solution)/shard_map/ppermute | solution.py:222
  6.8 68.6 %collective-permute-start.3 = (bf16[4,1,1,8,96,256]{5,4,3,2,1,0:T(8,128)(2,1)}, bf16[4,1,1,8,96,256]{5,4,3,2,1,0:T(8,128)(2,1)}, u32[]{:S(2)}, u32[]{:S(2)}) collective-permute-start(bf16[4,1,1,8,96,256]{5,4,3,2,1,0:T(8,128)(2,1)} %param.2), channel_id=1, source_target_pairs={{0,1},{1,2},{2,3},{3,0},{4,5},{5,6},{6,7},{7,4},{8,9},{9,10},{10,1... | collective-permute-start | bytes 4718600 | tf_op jit(solution)/shard_map/ppermute | solution.py:227
  8.6 3.0 copy-start
  43.1 32.4 %copy-start.10 = (bf16[4,1,1,8,96,256]{5,4,3,2,1,0:T(8,128)(2,1)}, bf16[4,1,1,8,96,256]{5,4,3,2,1,0:T(8,128)(2,1)S(1)}, u32[]{:S(2)}) copy-start(bf16[4,1,1,8,96,256]{5,4,3,2,1,0:T(8,128)(2,1)S(1)} %collective-permute-done.2) | copy-start | bytes 4718596
  83.0 3.5 copy-start.3
  94.1 3.6 copy-start.8
  96.5 3.2 copy-start.7
  97.8 2.4 copy-start.5
  101.9 1.6 copy-start.12
  103.5 179.3 %collective-permute-start.4 = (bf16[4,1,1,8,96,256]{5,4,3,0,2,1:T(8,128)(2,1)}, bf16[4,1,1,8,96,256]{5,4,3,0,2,1:T(8,128)(2,1)}, u32[]{:S(2)}, u32[]{:S(2)}) collective-permute-start(bf16[4,1,1,8,96,256]{5,4,3,0,2,1:T(8,128)(2,1)} %fusion.92), channel_id=1, source_target_pairs={{0,4},{4,8},{8,12},{12,0},{1,5},{5,9},{9,13},{13,1},{2,6},{6,10},{... | collective-permute-start | bytes 4718600 | tf_op jit(solution)/shard_map/ppermute | solution.py:227
  103.6 179.3 %collective-permute-start.5 = (bf16[4,1,1,8,96,256]{5,4,3,0,2,1:T(8,128)(2,1)}, bf16[4,1,1,8,96,256]{5,4,3,0,2,1:T(8,128)(2,1)}, u32[]{:S(2)}, u32[]{:S(2)}) collective-permute-start(bf16[4,1,1,8,96,256]{5,4,3,0,2,1:T(8,128)(2,1)} %fusion.93), channel_id=1, source_target_pairs={{4,0},{8,4},{12,8},{0,12},{5,1},{9,5},{13,9},{1,13},{6,2},{10,6},{... | collective-permute-start | bytes 4718600 | tf_op jit(solution)/shard_map/ppermute | solution.py:222
  105.3 177.5 %collective-permute-start.6 = (bf16[4,1,1,8,96,256]{5,4,3,0,2,1:T(8,128)(2,1)}, bf16[4,1,1,8,96,256]{5,4,3,0,2,1:T(8,128)(2,1)}, u32[]{:S(2)}, u32[]{:S(2)}) collective-permute-start(bf16[4,1,1,8,96,256]{5,4,3,0,2,1:T(8,128)(2,1)} %bitcast.55), channel_id=1, source_target_pairs={{0,1},{1,2},{2,3},{3,0},{4,5},{5,6},{6,7},{7,4},{8,9},{9,10},{10,1... | collective-permute-start | bytes 4718600 | tf_op jit(solution)/shard_map/ppermute | solution.py:227
  107.0 175.9 %collective-permute-start.7 = (bf16[4,1,1,8,96,256]{5,4,3,0,2,1:T(8,128)(2,1)}, bf16[4,1,1,8,96,256]{5,4,3,0,2,1:T(8,128)(2,1)}, u32[]{:S(2)}, u32[]{:S(2)}) collective-permute-start(bf16[4,1,1,8,96,256]{5,4,3,0,2,1:T(8,128)(2,1)} %bitcast.56), channel_id=1, source_target_pairs={{1,0},{2,1},{3,2},{0,3},{5,4},{6,5},{7,6},{4,7},{9,8},{10,9},{11,1... | collective-permute-start | bytes 4718600 | tf_op jit(solution)/shard_map/ppermute | solution.py:222
  109.6 89.2 %copy-start.9 = (bf16[4,8,96,256]{3,2,1,0:T(8,128)(2,1)S(1)}, bf16[4,8,96,256]{3,2,1,0:T(8,128)(2,1)}, u32[]{:S(2)}) copy-start(bf16[4,8,96,256]{3,2,1,0:T(8,128)(2,1)} %fusion.94) | copy-start | bytes 4718596
  243.0 39.9 %slice-start.2 = ((bf16[4,1,1,8,96,256]{5,4,3,0,2,1:T(8,128)(2,1)}), bf16[4,1,1,1,96,256]{5,4,3,0,2,1:T(8,128)(2,1)S(1)}, s32[]{:S(2)}) async-start(bf16[4,1,1,8,96,256]{5,4,3,0,2,1:T(8,128)(2,1)} %copy-done.7), calls=%async_computation.2 | async-start | bytes 393216 | tf_op jit(solution)/shard_map/jit(_roll_static)/slice | solution.py:287
  243.0 39.9 %slice-start.3 = ((bf16[4,1,1,8,96,256]{5,4,3,0,2,1:T(8,128)(2,1)}), bf16[4,1,1,1,96,256]{5,4,3,0,2,1:T(8,128)(2,1)S(1)}, s32[]{:S(2)}) async-start(bf16[4,1,1,8,96,256]{5,4,3,0,2,1:T(8,128)(2,1)} %copy-done.8), calls=%async_computation.3 | async-start | bytes 393216 | tf_op jit(solution)/shard_map/jit(_roll_static)/slice | solution.py:287
  243.0 48.7 %slice-start = ((s8[7077888]{0:T(1024)(128)(4,1)}), s8[2883584]{0:T(1024)(128)(4,1)S(1)}, s32[]{:S(2)}) async-start(s8[7077888]{0:T(1024)(128)(4,1)} %bitcast.378), calls=%async_computation | async-start | bytes 5767168
  282.9 8.7 %slice-start.1 = ((s8[7077888]{0:T(1024)(128)(4,1)}), s8[4194304]{0:T(1024)(128)(4,1)S(1)}, s32[]{:S(2)}) async-start(s8[7077888]{0:T(1024)(128)(4,1)} %bitcast.378), calls=%async_computation.1 | async-start | bytes 8388608
  292.2 39.3 %collective-permute-start.11 = (bf16[4,1,1,8,96,256]{5,4,3,0,2,1:T(8,128)(2,1)S(1)}, bf16[4,1,1,8,96,256]{5,4,3,0,2,1:T(8,128)(2,1)}, u32[]{:S(2)}, u32[]{:S(2)}) collective-permute-start(bf16[4,1,1,8,96,256]{5,4,3,0,2,1:T(8,128)(2,1)S(1)} %get-tuple-element.32), channel_id=1, source_target_pairs={{0,1},{1,2},{2,3},{3,0},{4,5},{5,6},{6,7},{7,4},{8,9},{9,10},{10,1... | collective-permute-start | bytes 4718600 | tf_op jit(solution)/shard_map/ppermute | solution.py:227
  293.1 69.8 %collective-permute-start.10 = (bf16[4,1,1,8,96,256]{5,4,3,0,2,1:T(8,128)(2,1)S(1)}, bf16[4,1,1,8,96,256]{5,4,3,0,2,1:T(8,128)(2,1)}, u32[]{:S(2)}, u32[]{:S(2)}) collective-permute-start(bf16[4,1,1,8,96,256]{5,4,3,0,2,1:T(8,128)(2,1)S(1)} %get-tuple-element.32), channel_id=1, source_target_pairs={{1,0},{2,1},{3,2},{0,3},{5,4},{6,5},{7,6},{4,7},{9,8},{10,9},{11,1... | collective-permute-start | bytes 4718600 | tf_op jit(solution)/shard_map/ppermute | solution.py:222
  296.3 68.7 %collective-permute-start.9 = (bf16[4,1,1,8,96,256]{5,4,3,0,2,1:T(8,128)(2,1)S(1)}, bf16[4,1,1,8,96,256]{5,4,3,0,2,1:T(8,128)(2,1)}, u32[]{:S(2)}, u32[]{:S(2)}) collective-permute-start(bf16[4,1,1,8,96,256]{5,4,3,0,2,1:T(8,128)(2,1)S(1)} %get-tuple-element.32), channel_id=1, source_target_pairs={{0,4},{4,8},{8,12},{12,0},{1,5},{5,9},{9,13},{13,1},{2,6},{6,10},{... | collective-permute-start | bytes 4718600 | tf_op jit(solution)/shard_map/ppermute | solution.py:227
  296.3 70.6 %collective-permute-start.8 = (bf16[4,1,1,8,96,256]{5,4,3,0,2,1:T(8,128)(2,1)S(1)}, bf16[4,1,1,8,96,256]{5,4,3,0,2,1:T(8,128)(2,1)}, u32[]{:S(2)}, u32[]{:S(2)}) collective-permute-start(bf16[4,1,1,8,96,256]{5,4,3,0,2,1:T(8,128)(2,1)S(1)} %get-tuple-element.32), channel_id=1, source_target_pairs={{4,0},{8,4},{12,8},{0,12},{5,1},{9,5},{13,9},{1,13},{6,2},{10,6},{... | collective-permute-start | bytes 4718600 | tf_op jit(solution)/shard_map/ppermute | solution.py:222
  299.8 1.4 copy-start.11
  302.6 69.0 %copy-start.4 = (f32[4,8,96,256]{3,2,1,0:T(8,128)}, f32[4,8,96,256]{3,2,1,0:T(8,128)S(1)}, u32[]{:S(2)}) copy-start(f32[4,8,96,256]{3,2,1,0:T(8,128)S(1)} %fusion.29) | copy-start | bytes 9437188
  368.9 1.9 copy-start.6
  370.8 1.4 copy-start.2
  450.4 3.4 copy-start.13
